TPU v7x, 256 devices: a whole 4x4x8 slice. The times are simulated.
256 devices in a mesh: energy: 16 (over z, core), block: 16 (over x, y).
Axes of the slice: x: 4, y: 4, z: 8, core: 2. Of those that a mesh axis runs over, the one named last changes fastest.
Arguments:
- g_lesser: float32 [2, 16, 4096, 256], P(None, 'energy', 'block'), may hold values from -0.75 to 0.75
- g_greater: float32 [2, 16, 4096, 256], P(None, 'energy', 'block'), may hold values from -0.75 to 0.75
- onsite: float32 [2, 16, 4096, 256], P(None, 'energy', 'block'), may hold values from -1 to 7
- lower: float32 [2, 4096, 256], P(None, 'block'), may hold values from -0.5 to 2.7
- upper: float32 [2, 4096, 256], P(None, 'block'), may hold values from -0.5 to 2.7
- rhs: float32 [2, 16, 4096, 128], P(None, 'energy', 'block'), may hold values from -16 to 16
Outputs:
- solution: float32 [2, 16, 4096, 128], P(None, 'energy', 'block')
All inputs are finite; a program needn't handle non-finite values.
Results may differ from a plain program's by a relative error of at most 0.0003.
Values sent between devices are 32-bit elements; how exact they have to be, the bound alone decides.
No kernel may reach another device: no remote copies, remote signals or barrier semaphores. Data moves between devices by JAX's collectives and lax.ppermute only.
A program may use at most 64 MiB of HBM per device.

v0:
```python
import jax
import jax.numpy as jnp
from jax import lax
from jax.experimental import pallas as pl
from jax.experimental.pallas import tpu as pltpu
from jax.sharding import PartitionSpec as P


F32 = jnp.float32
BF16 = jnp.bfloat16
VMEM_LIMIT = 28 << 20
GUESS = 0.2


def split(value):
    high = value.astype(BF16)
    return high, (value - high.astype(F32)).astype(BF16)


def left_side(pair):
    sides = []
    for value in (pair[0], pair[1], pair[0] + pair[1]):
        high, low = split(value)
        sides.append(jnp.concatenate([high, high, low], axis=1))
    return sides


def real_product(side, value):
    high, low = split(value)
    return jnp.dot(
        side, jnp.concatenate([high, low, high], axis=0), preferred_element_type=F32
    )


def multiply(left, pair):
    real = real_product(left[0], pair[0])
    imag = real_product(left[1], pair[1])
    both = real_product(left[2], pair[0] + pair[1])
    return real - imag, both - real - imag


def load(ref):
    return ref[0], ref[1]


def save(ref, pair):
    ref[0] = pair[0]
    ref[1] = pair[1]


def minus(a, b):
    return a[0] - b[0], a[1] - b[1]


def negative(a):
    return -a[0], -a[1]


def choose(flag, a, b):
    return jnp.where(flag, a[0], b[0]), jnp.where(flag, a[1], b[1])


def columns_of(pair, start, stop):
    return pair[0][:, start:stop], pair[1][:, start:stop]


def newton_inverse(diag):
    order = diag[0].shape[0]
    rows = lax.broadcasted_iota(jnp.int32, (order, order), 0)
    columns = lax.broadcasted_iota(jnp.int32, (order, order), 1)
    identity = (rows == columns).astype(F32)
    base = (identity - diag[0] * GUESS, diag[1] * (-GUESS))
    left = left_side(base)
    square = multiply(left, base)
    cube = multiply(left, square)
    return (
        (identity + base[0] + square[0] + cube[0]) * GUESS,
        (base[1] + square[1] + cube[1]) * GUESS,
    )


def convolve_kernel(g_ref, out_ref):
    energies = g_ref.shape[0]
    scale = energies**-0.5

    def rows_of(step, carry):
        here = pl.ds(pl.multiple_of(step * 8, 8), 8)
        for offset in range(energies):
            real = imag = None
            for e in range(offset, energies):
                lr, li = g_ref[e, 0, here, :], g_ref[e, 1, here, :]
                gr, gi = g_ref[e - offset, 2, here, :], g_ref[e - offset, 3, here, :]
                re, im = lr * gr - li * gi, lr * gi + li * gr
                real = re if real is None else real + re
                imag = im if imag is None else imag + im
            out_ref[offset, 0, here, :] = real * scale
            out_ref[offset, 1, here, :] = imag * scale
        return carry

    lax.fori_loop(0, g_ref.shape[2] // 8, rows_of, 0)


def first_kernel(onsite_ref, polar_ref, diag_ref, inverse_ref):
    shape = onsite_ref.shape[1:]
    diag = tuple(onsite_ref[c] - polar_ref[:, c].reshape(shape) for c in range(2))
    save(diag_ref, diag)
    save(inverse_ref, newton_inverse(diag))


def level0_kernel(
    core_ref, diag_ref, lower_ref, upper_ref, xl_ref, xr_ref, hl_ref, ol_ref, hr_ref, or_ref,
    d_ref, l_ref, alpha_ref, inverse_ref, tl_ref, tr_ref,
):
    flag = core_ref[0] > 0
    diag = load(diag_ref)
    before = multiply(left_side(load(lower_ref)), load(xl_ref))
    save(tl_ref, before)
    left = left_side(before)
    zh, zo = multiply(left, load(hl_ref)), multiply(left, load(ol_ref))
    diag = minus(diag, choose(flag, zo, zh))
    new_lower = negative(choose(flag, zh, zo))
    save(l_ref, new_lower)
    after = multiply(left_side(load(upper_ref)), load(xr_ref))
    save(tr_ref, after)
    diag = minus(diag, multiply(left_side(after), choose(flag, load(hr_ref), load(or_ref))))
    save(d_ref, diag)
    inverse = newton_inverse(diag)
    save(inverse_ref, inverse)
    save(alpha_ref, multiply(left_side(inverse), new_lower))


def level0_rest_kernel(
    core_ref, rhs_ref, inverse_ref, tl_ref, tr_ref, hr_ref, or_ref, rl_ref, rr_ref,
    u_ref, r_ref, beta_ref, rho_ref,
):
    flag = core_ref[0] > 0
    source = minus(load(rhs_ref), multiply(left_side(load(tl_ref)), load(rl_ref)))
    after = left_side(load(tr_ref))
    new_upper = negative(multiply(after, choose(flag, load(or_ref), load(hr_ref))))
    source = minus(source, multiply(after, load(rr_ref)))
    save(u_ref, new_upper)
    save(r_ref, source)
    left = left_side(load(inverse_ref))
    save(beta_ref, multiply(left, new_upper))
    save(rho_ref, multiply(left, source))


def level1_first_kernel(
    flag_ref, diag_ref, lower_ref, upper_ref, rhs_ref, pa_ref, pb_ref, pr_ref,
    d_ref, p_ref, r_ref,
):
    flag = flag_ref[0] > 0
    left = left_side(choose(flag, load(upper_ref), load(lower_ref)))
    za, zb = multiply(left, load(pa_ref)), multiply(left, load(pb_ref))
    save(d_ref, minus(load(diag_ref), choose(flag, za, zb)))
    save(p_ref, negative(choose(flag, zb, za)))
    save(r_ref, minus(load(rhs_ref), multiply(left, load(pr_ref))))


def level1_kernel(
    flag_ref, diag_ref, lower_ref, upper_ref, rhs_ref, p_ref, qa_ref, qb_ref, qr_ref,
    d_ref, l_ref, u_ref, r_ref, coef_ref,
):
    flag = flag_ref[0] > 0
    n = diag_ref.shape[1]
    left = left_side(choose(flag, load(lower_ref), load(upper_ref)))
    za, zb = multiply(left, load(qa_ref)), multiply(left, load(qb_ref))
    diag = minus(load(diag_ref), choose(flag, zb, za))
    save(d_ref, diag)
    new_p, new_q = load(p_ref), negative(choose(flag, za, zb))
    source = minus(load(rhs_ref), multiply(left, load(qr_ref)))
    new_upper, new_lower = choose(flag, new_p, new_q), choose(flag, new_q, new_p)
    save(l_ref, new_lower)
    save(u_ref, new_upper)
    save(r_ref, source)
    left = left_side(newton_inverse(diag))
    for start, part in ((0, new_lower), (n, new_upper), (2 * n, source)):
        z = multiply(left, part)
        coef_ref[0, :, start : start + part[0].shape[1]] = z[0]
        coef_ref[1, :, start : start + part[0].shape[1]] = z[1]


def level2_kernel(
    flag_ref, diag_ref, lower_ref, upper_ref, rhs_ref, cl_ref, cr_ref,
    d_ref, r_ref, w_ref, coef_ref,
):
    flag = flag_ref[0] > 0
    n = diag_ref.shape[1]
    diag, source = load(diag_ref), load(rhs_ref)
    before, after = load(cl_ref), load(cr_ref)
    left_l, left_u = left_side(load(lower_ref)), left_side(load(upper_ref))
    z = multiply(left_l, columns_of(before, n, None))
    diag = minus(diag, columns_of(z, 0, n))
    source = minus(source, columns_of(z, n, None))
    diag = minus(diag, multiply(left_u, columns_of(after, 0, n)))
    source = minus(source, multiply(left_u, columns_of(after, 2 * n, None)))
    left = [jnp.where(flag, u, l) for u, l in zip(left_u, left_l)]
    other = choose(flag, columns_of(after, n, 2 * n), columns_of(before, 0, n))
    coupling = negative(multiply(left, other))
    save(d_ref, diag)
    save(r_ref, source)
    save(w_ref, coupling)
    left = left_side(newton_inverse(diag))
    for start, part in ((0, coupling), (n, source)):
        z = multiply(left, part)
        coef_ref[0, :, start : start + part[0].shape[1]] = z[0]
        coef_ref[1, :, start : start + part[0].shape[1]] = z[1]


def last_kernel(diag_ref, rhs_ref, w_ref, coef_ref, out_ref):
    n = diag_ref.shape[1]
    z = multiply(left_side(load(w_ref)), load(coef_ref))
    diag = minus(load(diag_ref), columns_of(z, 0, n))
    source = minus(load(rhs_ref), columns_of(z, n, None))
    save(out_ref, multiply(left_side(newton_inverse(diag)), source))


def run(kernel, out_shapes, args, products, scalars=0):
    outs = [jax.ShapeDtypeStruct(shape, F32) for shape in out_shapes]
    specs = [pl.BlockSpec(memory_space=pltpu.SMEM)] * scalars
    specs += [pl.BlockSpec(memory_space=pltpu.VMEM)] * (len(args) - scalars)
    moved = sum(a.size * 4 for a in args) + sum(o.size * 4 for o in outs)
    return pl.pallas_call(
        kernel,
        out_shape=outs,
        in_specs=specs,
        out_specs=[pl.BlockSpec(memory_space=pltpu.VMEM)] * len(outs),
        compiler_params=pltpu.CompilerParams(vmem_limit_bytes=VMEM_LIMIT),
        cost_estimate=pl.CostEstimate(
            flops=int(products * 24 * 256**3), bytes_accessed=moved, transcendentals=0
        ),
    )(*args)


def program(g_lesser, g_greater, onsite, lower, upper, rhs):
    energies, blocks = lax.axis_size("energy"), lax.axis_size("block")
    block = lax.axis_index("block")
    n, columns = onsite.shape[-1], rhs.shape[-1]
    share = n // energies
    onsite, rhs = onsite[:, 0], rhs[:, 0]

    def send(value, pairs):
        return lax.ppermute(value, "block", pairs)

    def shift(value, steps):
        return send(value, [(b, b + steps) for b in range(max(0, -steps), min(blocks, blocks - steps))])

    def flag(condition):
        return condition.astype(jnp.int32).reshape(1)

    first_core = lax.axis_index("energy") % 2 == 0
    half = jnp.where(
        first_core,
        jnp.where(block > 0, lower, 0.0),
        jnp.where(block < blocks - 1, upper, 0.0),
    )
    half_left, half_right = shift(half, 1), shift(half, -1)
    pairs = jnp.concatenate([g_lesser[:, 0], g_greater[:, 0]], axis=0)
    pairs = pairs.reshape(4, energies, share, n).swapaxes(0, 1)
    pairs = lax.all_to_all(pairs, "energy", split_axis=0, concat_axis=0, tiled=True)
    (polar,) = run(convolve_kernel, [(energies, 2, share, n)], [pairs], 0.02)
    core_flag, right_first, low_half = flag(first_core), flag(block & 2 == 0), flag(block < blocks // 2)
    polar, half_left, half_right, core_flag, right_first, low_half = lax.optimization_barrier(
        (polar, half_left, half_right, core_flag, right_first, low_half)
    )
    polar = lax.all_to_all(polar, "energy", split_axis=0, concat_axis=0, tiled=True)
    other = [(e, e ^ 1) for e in range(energies)]
    other_left = lax.ppermute(half_left, "energy", other)
    other_right = lax.ppermute(half_right, "energy", other)
    rhs_left, rhs_right = shift(rhs, 1), shift(rhs, -1)
    polar, other_left, other_right, rhs_left, rhs_right = lax.optimization_barrier(
        (polar, other_left, other_right, rhs_left, rhs_right)
    )

    square, wide = (2, n, n), (2, n, 2 * n + columns)
    slim, tall = (2, n, n + columns), (2, n, columns)
    diag, inverse = run(first_kernel, [square, square], [onsite, polar], 2)
    inverse_left, inverse_right = shift(inverse, 1), shift(inverse, -1)
    diag, low, alpha, inverse, through_left, through_right = run(
        level0_kernel,
        [square] * 6,
        [core_flag, diag, lower, upper, inverse_left, inverse_right, half_left, other_left, half_right, other_right],
        8,
        1,
    )
    up, source, beta, rho = run(
        level0_rest_kernel,
        [square, tall, square, tall],
        [core_flag, rhs, inverse, through_left, through_right, half_right, other_right, rhs_left, rhs_right],
        3.5,
        1,
    )

    across = [(b, b ^ 2) for b in range(blocks)]
    hand_on = [(b, b - 4 if b & 2 else b + 4) for b in range(blocks)]
    hand_on = [(b, t) for b, t in hand_on if 0 <= t < blocks]
    far = [(b, b + 2 if b & 2 else b - 2) for b in range(blocks)]
    far = [(b, t) for b, t in far if 0 <= t < blocks]

    swapped = [send(alpha, across), send(beta, across), send(rho, across)]
    handed = [send(swapped[0], hand_on), send(swapped[1], hand_on), send(rho, far)]
    diag, coupling, source = run(
        level1_first_kernel,
        [square, square, tall],
        [right_first, diag, low, up, source, *swapped],
        2.5,
        1,
    )
    diag, low, up, source, coef = run(
        level1_kernel,
        [square, square, square, tall, wide],
        [right_first, diag, low, up, source, coupling, *handed],
        7,
        1,
    )

    coef_left, coef_right = shift(coef, 4), shift(coef, -4)
    diag, source, coupling, coef = run(
        level2_kernel,
        [square, tall, square, slim],
        [low_half, diag, low, up, source, coef_left, coef_right],
        7.5,
        1,
    )
    coef = send(coef, [(b, b ^ 8) for b in range(blocks)])
    (solution,) = run(last_kernel, [tall], [diag, source, coupling, coef], 4)
    return solution[:, None]


def solution(mesh):
    placed = (
        P(None, "energy", "block", None),
        P(None, "energy", "block", None),
        P(None, "energy", "block", None),
        P(None, "block", None),
        P(None, "block", None),
        P(None, "energy", "block", None),
    )
    return jax.shard_map(
        program,
        mesh=mesh,
        in_specs=placed,
        out_specs=P(None, "energy", "block", None),
        check_vma=False,
    )
```

profile of v0, /device:TPU:6, one launch (start us, length us, event | category | flops | bytes accessed | tf_op | source)
XLA Modules:
  0.0 197.9 jit_solution(1898922714429651473)
XLA Ops:
  0.0 2.3 %copy_bitcast_fusion = f32[16,4,16,256]{3,2,1,0:T(8,128)} fusion(f32[2,16,16,256]{3,2,1,0:T(8,128)} %bitcast.16, f32[2,16,16,256]{3,2,1,0:T(8,128)} %bitcast.17), kind=kLoop, calls=%fused_computation.1 | loop fusion | flops 262144 | bytes 2097152 | tf_op jit(solution)/shard_map/transpose | solution.py:259
  2.3 8.7 %all-to-all-start = ((f32[16,4,16,256]{3,2,1,0:T(8,128)}), f32[16,4,16,256]{3,2,1,0:T(8,128)S(1)}, u32[]{:S(2)}, u32[]{:S(2)}) async-start(f32[16,4,16,256]{3,2,1,0:T(8,128)} %copy_bitcast_fusion), calls=%async_computation | async-start | bytes 2097152 | tf_op jit(solution)/shard_map/all_to_all | solution.py:260
  11.9 5.2 %collective-permute-start.1 = (f32[2,256,256]{2,1,0:T(8,128)}, f32[2,256,256]{2,1,0:T(8,128)S(1)}, u32[]{:S(2)}, u32[]{:S(2)}) collective-permute-start(f32[2,256,256]{2,1,0:T(8,128)} %select_select_fusion), channel_id=1, source_target_pairs={{1,0},{2,1},{3,2},{4,3},{5,4},{6,5},{7,6},{8,7},{9,8},{10,9},{11,1... | collective-permute-start | bytes 1572872 | tf_op jit(solution)/shard_map/ppermute | solution.py:243
  19.0 18.4 %all-to-all-done.g_ref = f32[16,4,16,256]{3,2,1,0:T(8,128)S(1)} async-done(((f32[16,4,16,256]{3,2,1,0:T(8,128)}), f32[16,4,16,256]{3,2,1,0:T(8,128)S(1)}, u32[]{:S(2)}, u32[]{:S(2)}) %all-to-all-start) | async-done | bytes 1048608 | tf_op jit(solution)/shard_map/all_to_all | solution.py:260
  39.1 4.9 %all-to-all-start.1 = ((f32[16,2,16,256]{3,2,1,0:T(8,128)}), f32[16,2,16,256]{3,2,1,0:T(8,128)S(1)}, u32[]{:S(2)}, u32[]{:S(2)}) async-start(f32[16,2,16,256]{3,2,1,0:T(8,128)} %shard_map.64), calls=%async_computation.1 | async-start | bytes 1048576 | tf_op jit(solution)/shard_map/all_to_all | solution.py:266
  44.6 5.2 %collective-permute-start.5 = (f32[2,256,128]{2,1,0:T(8,128)S(1)}, f32[2,256,128]{2,1,0:T(8,128)S(1)}, u32[]{:S(2)}, u32[]{:S(2)}) collective-permute-start(f32[2,256,128]{2,1,0:T(8,128)S(1)} %bitcast.13), channel_id=1, source_target_pairs={{1,0},{2,1},{3,2},{4,3},{5,4},{6,5},{7,6},{8,7},{9,8},{10,9},{11,1... | collective-permute-start | bytes 786440 | tf_op jit(solution)/shard_map/ppermute | solution.py:243
  51.8 4.2 %collective-permute-done.5.rr_ref = f32[2,256,128]{2,1,0:T(8,128)S(1)} collective-permute-done((f32[2,256,128]{2,1,0:T(8,128)S(1)}, f32[2,256,128]{2,1,0:T(8,128)S(1)}, u32[]{:S(2)}, u32[]{:S(2)}) %collective-permute-start.5) | collective-permute-done | bytes 262176 | tf_op jit(solution)/shard_map/ppermute | solution.py:243
  56.7 5.5 %collective-permute-done.4.rl_ref = f32[2,256,128]{2,1,0:T(8,128)S(1)} collective-permute-done((f32[2,256,128]{2,1,0:T(8,128)S(1)}, f32[2,256,128]{2,1,0:T(8,128)S(1)}, u32[]{:S(2)}, u32[]{:S(2)}) %collective-permute-start.4) | collective-permute-done | bytes 262176 | tf_op jit(solution)/shard_map/ppermute | solution.py:243
  66.6 3.9 %collective-permute-start.6 = (f32[2,256,256]{2,1,0:T(8,128)S(1)}, f32[2,256,256]{2,1,0:T(8,128)S(1)}, u32[]{:S(2)}, u32[]{:S(2)}) collective-permute-start(f32[2,256,256]{2,1,0:T(8,128)S(1)} %get-tuple-element.48), channel_id=1, source_target_pairs={{0,1},{1,2},{2,3},{3,4},{4,5},{5,6},{6,7},{7,8},{8,9},{9,10},{10,1... | collective-permute-start | bytes 1572872 | tf_op jit(solution)/shard_map/ppermute | solution.py:243
  70.6 9.1 %collective-permute-done.7.xr_ref = f32[2,256,256]{2,1,0:T(8,128)S(1)} collective-permute-done((f32[2,256,256]{2,1,0:T(8,128)S(1)}, f32[2,256,256]{2,1,0:T(8,128)S(1)}, u32[]{:S(2)}, u32[]{:S(2)}) %collective-permute-start.7) | collective-permute-done | bytes 524320 | tf_op jit(solution)/shard_map/ppermute | solution.py:243
  79.7 5.7 %collective-permute-done.6.xl_ref = f32[2,256,256]{2,1,0:T(8,128)S(1)} collective-permute-done((f32[2,256,256]{2,1,0:T(8,128)S(1)}, f32[2,256,256]{2,1,0:T(8,128)S(1)}, u32[]{:S(2)}, u32[]{:S(2)}) %collective-permute-start.6) | collective-permute-done | bytes 524320 | tf_op jit(solution)/shard_map/ppermute | solution.py:243
  85.4 4.5 %shard_map.66 = (f32[2,256,256]{2,1,0:T(8,128)S(1)}, f32[2,256,256]{2,1,0:T(8,128)S(1)}, f32[2,256,256]{2,1,0:T(8,128)S(1)}, f32[2,256,256]{2,1,0:T(8,128)S(1)},...) custom-call(s32[1]{0:T(128)} %bitcast.3.core_ref, f32[2,256,256]{2,1,0:T(8,128)S(1)} %get-tuple-element.47.diag_ref, ...), custom_call_target="tpu_custom_call" | custom-call | flops 3221225472 | bytes 7864324 | tf_op jit(solution)/shard_map/pallas_call | solution.py:223
  91.9 3.5 %collective-permute-start.8 = (f32[2,256,256]{2,1,0:T(8,128)S(1)}, f32[2,256,256]{2,1,0:T(8,128)S(1)}, u32[]{:S(2)}, u32[]{:S(2)}) collective-permute-start(f32[2,256,256]{2,1,0:T(8,128)S(1)} %get-tuple-element.60), channel_id=1, source_target_pairs={{0,2},{1,3},{2,0},{3,1},{4,6},{5,7},{6,4},{7,5},{8,10},{9,11},{10,... | collective-permute-start | bytes 1572872 | tf_op jit(solution)/shard_map/ppermute | solution.py:243
  95.4 12.8 %collective-permute-done.9.pb_ref = f32[2,256,256]{2,1,0:T(8,128)S(1)} collective-permute-done((f32[2,256,256]{2,1,0:T(8,128)S(1)}, f32[2,256,256]{2,1,0:T(8,128)S(1)}, u32[]{:S(2)}, u32[]{:S(2)}) %collective-permute-start.9) | collective-permute-done | bytes 524320 | tf_op jit(solution)/shard_map/ppermute | solution.py:243
  109.5 9.0 %collective-permute-done.8.pa_ref = f32[2,256,256]{2,1,0:T(8,128)S(1)} collective-permute-done((f32[2,256,256]{2,1,0:T(8,128)S(1)}, f32[2,256,256]{2,1,0:T(8,128)S(1)}, u32[]{:S(2)}, u32[]{:S(2)}) %collective-permute-start.8) | collective-permute-done | bytes 524320 | tf_op jit(solution)/shard_map/ppermute | solution.py:243
  121.4 6.2 %collective-permute-start.13 = (f32[2,256,128]{2,1,0:T(8,128)S(1)}, f32[2,256,128]{2,1,0:T(8,128)S(1)}, u32[]{:S(2)}, u32[]{:S(2)}) collective-permute-start(f32[2,256,128]{2,1,0:T(8,128)S(1)} %get-tuple-element.62), channel_id=1, source_target_pairs={{2,4},{3,5},{4,2},{5,3},{6,8},{7,9},{8,6},{9,7},{10,12},{11,13},{1... | collective-permute-start | bytes 786440 | tf_op jit(solution)/shard_map/ppermute | solution.py:243
  127.6 6.8 %collective-permute-done.10.pr_ref = f32[2,256,128]{2,1,0:T(8,128)S(1)} collective-permute-done((f32[2,256,128]{2,1,0:T(8,128)S(1)}, f32[2,256,128]{2,1,0:T(8,128)S(1)}, u32[]{:S(2)}, u32[]{:S(2)}) %collective-permute-start.10) | collective-permute-done | bytes 262176 | tf_op jit(solution)/shard_map/ppermute | solution.py:243
  135.7 3.4 %shard_map.69 = (f32[2,256,256]{2,1,0:T(8,128)S(1)}, f32[2,256,256]{2,1,0:T(8,128)S(1)}, f32[2,256,256]{2,1,0:T(8,128)S(1)}, f32[2,256,128]{2,1,0:T(8,128)S(1)}, f32[2,256,640]{2,1,0:T(8,128)S(1)}) custom-call(s32[1]{0:T(128)} %bitcast.4.flag_ref, f32[2,256,256]{2,1,0:T(8,128)S(1)} %get-tuple-element.63.diag_ref, ...), custom_call_target="tpu_custom_call" | custom-call | flops 2818572288 | bytes 6815748 | tf_op jit(solution)/shard_map/pallas_call | solution.py:223
  139.0 4.4 %collective-permute-start.15 = (f32[2,256,640]{2,1,0:T(8,128)S(1)}, f32[2,256,640]{2,1,0:T(8,128)S(1)}, u32[]{:S(2)}, u32[]{:S(2)}) collective-permute-start(f32[2,256,640]{2,1,0:T(8,128)S(1)} %get-tuple-element.70), channel_id=1, source_target_pairs={{4,0},{5,1},{6,2},{7,3},{8,4},{9,5},{10,6},{11,7},{12,8},{13,9},{1... | collective-permute-start | bytes 3932168 | tf_op jit(solution)/shard_map/ppermute | solution.py:243
  144.7 24.9 %collective-permute-done.15.cr_ref = f32[2,256,640]{2,1,0:T(8,128)S(1)} collective-permute-done((f32[2,256,640]{2,1,0:T(8,128)S(1)}, f32[2,256,640]{2,1,0:T(8,128)S(1)}, u32[]{:S(2)}, u32[]{:S(2)}) %collective-permute-start.15) | collective-permute-done | bytes 1310752 | tf_op jit(solution)/shard_map/ppermute | solution.py:243
  169.5 4.2 %collective-permute-done.14.cl_ref = f32[2,256,640]{2,1,0:T(8,128)S(1)} collective-permute-done((f32[2,256,640]{2,1,0:T(8,128)S(1)}, f32[2,256,640]{2,1,0:T(8,128)S(1)}, u32[]{:S(2)}, u32[]{:S(2)}) %collective-permute-start.14) | collective-permute-done | bytes 1310752 | tf_op jit(solution)/shard_map/ppermute | solution.py:243
  173.7 3.5 %shard_map.70 = (f32[2,256,256]{2,1,0:T(8,128)S(1)}, f32[2,256,128]{2,1,0:T(8,128)S(1)}, f32[2,256,256]{2,1,0:T(8,128)S(1)}, f32[2,256,384]{2,1,0:T(8,128)S(1)}) custom-call(s32[1]{0:T(128)} %bitcast.5.flag_ref, f32[2,256,256]{2,1,0:T(8,128)S(1)} %get-tuple-element.66.diag_ref, f32[2,256,256]{2,1,0:T(8,128)S(1)} %get-tuple-element.67.lower_ref, ...), custom_call_target="tpu_custom_call" | custom-call | flops 3019898880 | bytes 6553604 | tf_op jit(solution)/shard_map/pallas_call | solution.py:223
  178.1 17.1 %collective-permute-done.16.coef_ref = f32[2,256,384]{2,1,0:T(8,128)S(1)} collective-permute-done((f32[2,256,384]{2,1,0:T(8,128)S(1)}, f32[2,256,384]{2,1,0:T(8,128)S(1)}, u32[]{:S(2)}, u32[]{:S(2)}) %collective-permute-start.16) | collective-permute-done | bytes 786464 | tf_op jit(solution)/shard_map/ppermute | solution.py:243
  195.2 2.7 %shard_map.71 = f32[2,256,128]{2,1,0:T(8,128)} custom-call(f32[2,256,256]{2,1,0:T(8,128)S(1)} %get-tuple-element.71.diag_ref, f32[2,256,128]{2,1,0:T(8,128)S(1)} %get-tuple-element.72.rhs_ref, f32[2,256,256]{2,1,0:T(8,128)S(1)} %get-tuple-element.73.w_ref, f32[2,256,384]{2,1,0:T(8,128)S(1)} %collective-permute-done.16.coef_ref), custom_call_target="tpu_custom_call" | custom-call | flops 1610612736 | bytes 2359296 | tf_op jit(solution)/shard_map/pallas_call | solution.py:223
  (44 shorter events, 21.6 us)
Async XLA Ops:
  2.3 8.7 %copy-start = (f32[2,256,256]{2,1,0:T(8,128)S(1)}, f32[2,256,256]{2,1,0:T(8,128)}, u32[]{:S(2)}) copy-start(f32[2,256,256]{2,1,0:T(8,128)} %lower_ref.1) | copy-start | bytes 1572868
  2.3 8.7 %copy-start.1 = (f32[2,256,256]{2,1,0:T(8,128)S(1)}, f32[2,256,256]{2,1,0:T(8,128)}, u32[]{:S(2)}) copy-start(f32[2,256,256]{2,1,0:T(8,128)} %upper_ref.1) | copy-start | bytes 1572868
  2.3 35.2 %all-to-all-start = ((f32[16,4,16,256]{3,2,1,0:T(8,128)}), f32[16,4,16,256]{3,2,1,0:T(8,128)S(1)}, u32[]{:S(2)}, u32[]{:S(2)}) async-start(f32[16,4,16,256]{3,2,1,0:T(8,128)} %copy_bitcast_fusion), calls=%async_computation | async-start | bytes 2097152 | tf_op jit(solution)/shard_map/all_to_all | solution.py:260
  11.9 27.2 %collective-permute-start.1 = (f32[2,256,256]{2,1,0:T(8,128)}, f32[2,256,256]{2,1,0:T(8,128)S(1)}, u32[]{:S(2)}, u32[]{:S(2)}) collective-permute-start(f32[2,256,256]{2,1,0:T(8,128)} %select_select_fusion), channel_id=1, source_target_pairs={{1,0},{2,1},{3,2},{4,3},{5,4},{6,5},{7,6},{8,7},{9,8},{10,9},{11,1... | collective-permute-start | bytes 1572872 | tf_op jit(solution)/shard_map/ppermute | solution.py:243
  17.1 22.0 %collective-permute-start = (f32[2,256,256]{2,1,0:T(8,128)}, f32[2,256,256]{2,1,0:T(8,128)}, u32[]{:S(2)}, u32[]{:S(2)}) collective-permute-start(f32[2,256,256]{2,1,0:T(8,128)} %select_select_fusion), channel_id=1, source_target_pairs={{0,1},{1,2},{2,3},{3,4},{4,5},{5,6},{6,7},{7,8},{8,9},{9,10},{10,1... | collective-permute-start | bytes 1572872 | tf_op jit(solution)/shard_map/ppermute | solution.py:243
  19.0 25.6 %copy-start.5 = (f32[2,1,256,128]{3,2,1,0:T(8,128)S(1)}, f32[2,1,256,128]{3,2,1,0:T(8,128)}, u32[]{:S(2)}) copy-start(f32[2,1,256,128]{3,2,1,0:T(8,128)} %param.11) | copy-start | bytes 786436
  19.0 44.7 %copy-start.2 = (f32[2,1,256,256]{3,2,1,0:T(8,128)S(1)}, f32[2,1,256,256]{3,2,1,0:T(8,128)}, u32[]{:S(2)}) copy-start(f32[2,1,256,256]{3,2,1,0:T(8,128)} %param.8) | copy-start | bytes 1572868
  39.1 24.6 %all-to-all-start.1 = ((f32[16,2,16,256]{3,2,1,0:T(8,128)}), f32[16,2,16,256]{3,2,1,0:T(8,128)S(1)}, u32[]{:S(2)}, u32[]{:S(2)}) async-start(f32[16,2,16,256]{3,2,1,0:T(8,128)} %shard_map.64), calls=%async_computation.1 | async-start | bytes 1048576 | tf_op jit(solution)/shard_map/all_to_all | solution.py:266
  44.0 18.9 %collective-permute-start.2 = (f32[2,256,256]{2,1,0:T(8,128)}, f32[2,256,256]{2,1,0:T(8,128)S(1)}, u32[]{:S(2)}, u32[]{:S(2)}) collective-permute-start(f32[2,256,256]{2,1,0:T(8,128)} %collective-permute-done.hl_ref), channel_id=1, source_target_pairs={{0,16},{16,0},{32,48},{48,32},{64,80},{80,64},{96,112},{112,96},{1... | collective-permute-start | bytes 1572872 | tf_op jit(solution)/shard_map/ppermute | solution.py:268
  44.5 19.2 %collective-permute-start.3 = (f32[2,256,256]{2,1,0:T(8,128)S(1)}, f32[2,256,256]{2,1,0:T(8,128)S(1)}, u32[]{:S(2)}, u32[]{:S(2)}) collective-permute-start(f32[2,256,256]{2,1,0:T(8,128)S(1)} %collective-permute-done.1.hr_ref), channel_id=1, source_target_pairs={{0,16},{16,0},{32,48},{48,32},{64,80},{80,64},{96,112},{112,96},{1... | collective-permute-start | bytes 1572872 | tf_op jit(solution)/shard_map/ppermute | solution.py:269
  44.6 11.3 %collective-permute-start.5 = (f32[2,256,128]{2,1,0:T(8,128)S(1)}, f32[2,256,128]{2,1,0:T(8,128)S(1)}, u32[]{:S(2)}, u32[]{:S(2)}) collective-permute-start(f32[2,256,128]{2,1,0:T(8,128)S(1)} %bitcast.13), channel_id=1, source_target_pairs={{1,0},{2,1},{3,2},{4,3},{5,4},{6,5},{7,6},{8,7},{9,8},{10,9},{11,1... | collective-permute-start | bytes 786440 | tf_op jit(solution)/shard_map/ppermute | solution.py:243
  49.8 12.3 %collective-permute-start.4 = (f32[2,256,128]{2,1,0:T(8,128)S(1)}, f32[2,256,128]{2,1,0:T(8,128)S(1)}, u32[]{:S(2)}, u32[]{:S(2)}) collective-permute-start(f32[2,256,128]{2,1,0:T(8,128)S(1)} %bitcast.14), channel_id=1, source_target_pairs={{0,1},{1,2},{2,3},{3,4},{4,5},{5,6},{6,7},{7,8},{8,9},{9,10},{10,1... | collective-permute-start | bytes 786440 | tf_op jit(solution)/shard_map/ppermute | solution.py:243
  63.7 21.7 %copy-start.4 = (f32[2,256,256]{2,1,0:T(8,128)S(1)}, f32[2,256,256]{2,1,0:T(8,128)}, u32[]{:S(2)}) copy-start(f32[2,256,256]{2,1,0:T(8,128)} %copy-done.3) | copy-start | bytes 1572868
  64.7 15.0 %collective-permute-start.7 = (f32[2,256,256]{2,1,0:T(8,128)S(1)}, f32[2,256,256]{2,1,0:T(8,128)S(1)}, u32[]{:S(2)}, u32[]{:S(2)}) collective-permute-start(f32[2,256,256]{2,1,0:T(8,128)S(1)} %get-tuple-element.48), channel_id=1, source_target_pairs={{1,0},{2,1},{3,2},{4,3},{5,4},{6,5},{7,6},{8,7},{9,8},{10,9},{11,1... | collective-permute-start | bytes 1572872 | tf_op jit(solution)/shard_map/ppermute | solution.py:243
  66.6 18.7 %collective-permute-start.6 = (f32[2,256,256]{2,1,0:T(8,128)S(1)}, f32[2,256,256]{2,1,0:T(8,128)S(1)}, u32[]{:S(2)}, u32[]{:S(2)}) collective-permute-start(f32[2,256,256]{2,1,0:T(8,128)S(1)} %get-tuple-element.48), channel_id=1, source_target_pairs={{0,1},{1,2},{2,3},{3,4},{4,5},{5,6},{6,7},{7,8},{8,9},{9,10},{10,1... | collective-permute-start | bytes 1572872 | tf_op jit(solution)/shard_map/ppermute | solution.py:243
  91.8 16.4 %collective-permute-start.9 = (f32[2,256,256]{2,1,0:T(8,128)S(1)}, f32[2,256,256]{2,1,0:T(8,128)S(1)}, u32[]{:S(2)}, u32[]{:S(2)}) collective-permute-start(f32[2,256,256]{2,1,0:T(8,128)S(1)} %get-tuple-element.61), channel_id=1, source_target_pairs={{0,2},{1,3},{2,0},{3,1},{4,6},{5,7},{6,4},{7,5},{8,10},{9,11},{10,... | collective-permute-start | bytes 1572872 | tf_op jit(solution)/shard_map/ppermute | solution.py:243
  91.9 26.6 %collective-permute-start.8 = (f32[2,256,256]{2,1,0:T(8,128)S(1)}, f32[2,256,256]{2,1,0:T(8,128)S(1)}, u32[]{:S(2)}, u32[]{:S(2)}) collective-permute-start(f32[2,256,256]{2,1,0:T(8,128)S(1)} %get-tuple-element.60), channel_id=1, source_target_pairs={{0,2},{1,3},{2,0},{3,1},{4,6},{5,7},{6,4},{7,5},{8,10},{9,11},{10,... | collective-permute-start | bytes 1572872 | tf_op jit(solution)/shard_map/ppermute | solution.py:243
  108.2 27.4 %collective-permute-start.12 = (f32[2,256,256]{2,1,0:T(8,128)S(1)}, f32[2,256,256]{2,1,0:T(8,128)S(1)}, u32[]{:S(2)}, u32[]{:S(2)}) collective-permute-start(f32[2,256,256]{2,1,0:T(8,128)S(1)} %collective-permute-done.9.pb_ref), channel_id=1, source_target_pairs={{0,4},{1,5},{4,8},{5,9},{6,2},{7,3},{8,12},{9,13},{10,6},{11,7},{1... | collective-permute-start | bytes 1572872 | tf_op jit(solution)/shard_map/ppermute | solution.py:243
  118.5 17.1 %collective-permute-start.11 = (f32[2,256,256]{2,1,0:T(8,128)S(1)}, f32[2,256,256]{2,1,0:T(8,128)S(1)}, u32[]{:S(2)}, u32[]{:S(2)}) collective-permute-start(f32[2,256,256]{2,1,0:T(8,128)S(1)} %collective-permute-done.8.pa_ref), channel_id=1, source_target_pairs={{0,4},{1,5},{4,8},{5,9},{6,2},{7,3},{8,12},{9,13},{10,6},{11,7},{1... | collective-permute-start | bytes 1572872 | tf_op jit(solution)/shard_map/ppermute | solution.py:243
  119.8 14.6 %collective-permute-start.10 = (f32[2,256,128]{2,1,0:T(8,128)S(1)}, f32[2,256,128]{2,1,0:T(8,128)S(1)}, u32[]{:S(2)}, u32[]{:S(2)}) collective-permute-start(f32[2,256,128]{2,1,0:T(8,128)S(1)} %get-tuple-element.62), channel_id=1, source_target_pairs={{0,2},{1,3},{2,0},{3,1},{4,6},{5,7},{6,4},{7,5},{8,10},{9,11},{10,... | collective-permute-start | bytes 786440 | tf_op jit(solution)/shard_map/ppermute | solution.py:243
  121.4 14.3 %collective-permute-start.13 = (f32[2,256,128]{2,1,0:T(8,128)S(1)}, f32[2,256,128]{2,1,0:T(8,128)S(1)}, u32[]{:S(2)}, u32[]{:S(2)}) collective-permute-start(f32[2,256,128]{2,1,0:T(8,128)S(1)} %get-tuple-element.62), channel_id=1, source_target_pairs={{2,4},{3,5},{4,2},{5,3},{6,8},{7,9},{8,6},{9,7},{10,12},{11,13},{1... | collective-permute-start | bytes 786440 | tf_op jit(solution)/shard_map/ppermute | solution.py:243
  139.0 30.5 %collective-permute-start.15 = (f32[2,256,640]{2,1,0:T(8,128)S(1)}, f32[2,256,640]{2,1,0:T(8,128)S(1)}, u32[]{:S(2)}, u32[]{:S(2)}) collective-permute-start(f32[2,256,640]{2,1,0:T(8,128)S(1)} %get-tuple-element.70), channel_id=1, source_target_pairs={{4,0},{5,1},{6,2},{7,3},{8,4},{9,5},{10,6},{11,7},{12,8},{13,9},{1... | collective-permute-start | bytes 3932168 | tf_op jit(solution)/shard_map/ppermute | solution.py:243
  143.4 30.3 %collective-permute-start.14 = (f32[2,256,640]{2,1,0:T(8,128)S(1)}, f32[2,256,640]{2,1,0:T(8,128)S(1)}, u32[]{:S(2)}, u32[]{:S(2)}) collective-permute-start(f32[2,256,640]{2,1,0:T(8,128)S(1)} %get-tuple-element.70), channel_id=1, source_target_pairs={{0,4},{1,5},{2,6},{3,7},{4,8},{5,9},{6,10},{7,11},{8,12},{9,13},{1... | collective-permute-start | bytes 3932168 | tf_op jit(solution)/shard_map/ppermute | solution.py:243
  177.2 18.0 %collective-permute-start.16 = (f32[2,256,384]{2,1,0:T(8,128)S(1)}, f32[2,256,384]{2,1,0:T(8,128)S(1)}, u32[]{:S(2)}, u32[]{:S(2)}) collective-permute-start(f32[2,256,384]{2,1,0:T(8,128)S(1)} %get-tuple-element.74), channel_id=1, source_target_pairs={{0,8},{1,9},{2,10},{3,11},{4,12},{5,13},{6,14},{7,15},{8,0},{9,1},... | collective-permute-start | bytes 2359304 | tf_op jit(solution)/shard_map/ppermute | solution.py:243
  (5 other events, 11.3 us)
where the time goes:
time: 199 us; the launch traced here: 198 us
  waiting for transfers between devices  118 us (59%)
  starting transfers between devices  54.8 us (28%)
  Pallas kernels  19.8 us (10%)
  other arithmetic  3.13 us (2%)
  local copies, waits for them, and re-layouts  2.25 us (1%)
    ppermute x15, waiting for transfers between devices, send(): return lax.ppermute(value, 'block', pairs)  99.2 us
    ppermute x15, starting transfers between devices, send(): return lax.ppermute(value, 'block', pairs)  40.5 us
    pallas_call x8, Pallas kernels, run(): pl.pallas_call(kernel, out_shape=outs, in_specs=specs, out_specs=[pl.Bloc...  19.8 us
    all_to_all x1, waiting for transfers between devices, program(): lax.all_to_all(pairs, 'energy', split_axis=0, concat_axis=0, tiled=True)  18.4 us
    all_to_all x1, starting transfers between devices, program(): lax.all_to_all(pairs, 'energy', split_axis=0, concat_axis=0, tiled=True)  8.7 us
    all_to_all x1, starting transfers between devices, program(): lax.all_to_all(polar, 'energy', split_axis=0, concat_axis=0, tiled=True)  4.93 us
  transfers between devices with their start and end apart: 19, of which 11 were waited for; matrix products, arithmetic and copies ran while one was open for 0% of the time, Pallas kernels for 1%

commit v1 on v0

--- a/solution.py
+++ b/solution.py
@@ -32,13 +32,25 @@
     )
 
 
-def multiply(left, pair):
+def wide_product(left, pair):
     real = real_product(left[0], pair[0])
     imag = real_product(left[1], pair[1])
     both = real_product(left[2], pair[0] + pair[1])
     return real - imag, both - real - imag
 
 
+def multiply(left, pair):
+    columns = pair[0].shape[1]
+    if columns > 128:
+        return wide_product(left, pair)
+    full = real_product(jnp.concatenate(left[:2], axis=0), jnp.concatenate(pair, axis=1))
+    rows = left[0].shape[0]
+    return (
+        full[:rows, :columns] - full[rows:, columns:],
+        full[:rows, columns:] + full[rows:, :columns],
+    )
+
+
 def load(ref):
     return ref[0], ref[1]
 
@@ -64,12 +76,16 @@
     return pair[0][:, start:stop], pair[1][:, start:stop]
 
 
-def newton_inverse(diag):
+def step_matrix(diag):
     order = diag[0].shape[0]
     rows = lax.broadcasted_iota(jnp.int32, (order, order), 0)
     columns = lax.broadcasted_iota(jnp.int32, (order, order), 1)
     identity = (rows == columns).astype(F32)
-    base = (identity - diag[0] * GUESS, diag[1] * (-GUESS))
+    return identity, (identity - diag[0] * GUESS, diag[1] * (-GUESS))
+
+
+def newton_inverse(diag):
+    identity, base = step_matrix(diag)
     left = left_side(base)
     square = multiply(left, base)
     cube = multiply(left, square)
@@ -79,25 +95,45 @@
     )
 
 
+def newton_solve(diag, source):
+    left = left_side(step_matrix(diag)[1])
+    value = source
+    for _ in range(3):
+        z = wide_product(left, value)
+        value = source[0] + z[0], source[1] + z[1]
+    return value[0] * GUESS, value[1] * GUESS
+
+
 def convolve_kernel(g_ref, out_ref):
     energies = g_ref.shape[0]
     scale = energies**-0.5
-
-    def rows_of(step, carry):
-        here = pl.ds(pl.multiple_of(step * 8, 8), 8)
-        for offset in range(energies):
-            real = imag = None
-            for e in range(offset, energies):
-                lr, li = g_ref[e, 0, here, :], g_ref[e, 1, here, :]
-                gr, gi = g_ref[e - offset, 2, here, :], g_ref[e - offset, 3, here, :]
-                re, im = lr * gr - li * gi, lr * gi + li * gr
-                real = re if real is None else real + re
-                imag = im if imag is None else imag + im
-            out_ref[offset, 0, here, :] = real * scale
-            out_ref[offset, 1, here, :] = imag * scale
-        return carry
-
-    lax.fori_loop(0, g_ref.shape[2] // 8, rows_of, 0)
+    here = pl.ds(pl.multiple_of(pl.program_id(0) * 8, 8), 8)
+    for offset in range(energies):
+        real = imag = None
+        for e in range(offset, energies):
+            lr, li = g_ref[e, 0, here, :], g_ref[e, 1, here, :]
+            gr, gi = g_ref[e - offset, 2, here, :], g_ref[e - offset, 3, here, :]
+            re, im = lr * gr - li * gi, lr * gi + li * gr
+            real = re if real is None else real + re
+            imag = im if imag is None else imag + im
+        out_ref[offset, 0] = real * scale
+        out_ref[offset, 1] = imag * scale
+
+
+def convolve(pairs):
+    energies, _, share, n = pairs.shape
+    return pl.pallas_call(
+        convolve_kernel,
+        name="convolve",
+        grid=(share // 8,),
+        out_shape=jax.ShapeDtypeStruct((energies, 2, share, n), F32),
+        in_specs=[pl.BlockSpec(memory_space=pltpu.VMEM)],
+        out_specs=pl.BlockSpec((energies, 2, 8, n), lambda r: (0, 0, r, 0)),
+        compiler_params=pltpu.CompilerParams(vmem_limit_bytes=VMEM_LIMIT),
+        cost_estimate=pl.CostEstimate(
+            flops=4 * energies**2 * share * n, bytes_accessed=6 * pairs.size, transcendentals=0
+        ),
+    )(pairs)
 
 
 def first_kernel(onsite_ref, polar_ref, diag_ref, inverse_ref):
@@ -157,22 +193,33 @@
     save(r_ref, minus(load(rhs_ref), multiply(left, load(pr_ref))))
 
 
+def level1_middle_kernel(
+    flag_ref, diag_ref, lower_ref, upper_ref, rhs_ref, qa_ref, qr_ref, d_ref, q_ref, r_ref
+):
+    flag = flag_ref[0] > 0
+    left = left_side(choose(flag, load(lower_ref), load(upper_ref)))
+    za = multiply(left, load(qa_ref))
+    diag = load(diag_ref)
+    save(d_ref, choose(flag, diag, minus(diag, za)))
+    save(q_ref, negative(za))
+    save(r_ref, minus(load(rhs_ref), multiply(left, load(qr_ref))))
+
+
 def level1_kernel(
-    flag_ref, diag_ref, lower_ref, upper_ref, rhs_ref, p_ref, qa_ref, qb_ref, qr_ref,
-    d_ref, l_ref, u_ref, r_ref, coef_ref,
+    flag_ref, diag_ref, lower_ref, upper_ref, rhs_ref, p_ref, q_ref, qb_ref,
+    d_ref, l_ref, u_ref, coef_ref,
 ):
     flag = flag_ref[0] > 0
     n = diag_ref.shape[1]
     left = left_side(choose(flag, load(lower_ref), load(upper_ref)))
-    za, zb = multiply(left, load(qa_ref)), multiply(left, load(qb_ref))
-    diag = minus(load(diag_ref), choose(flag, zb, za))
+    zb = multiply(left, load(qb_ref))
+    diag = load(diag_ref)
+    diag = choose(flag, minus(diag, zb), diag)
     save(d_ref, diag)
-    new_p, new_q = load(p_ref), negative(choose(flag, za, zb))
-    source = minus(load(rhs_ref), multiply(left, load(qr_ref)))
+    new_p, new_q, source = load(p_ref), choose(flag, load(q_ref), negative(zb)), load(rhs_ref)
     new_upper, new_lower = choose(flag, new_p, new_q), choose(flag, new_q, new_p)
     save(l_ref, new_lower)
     save(u_ref, new_upper)
-    save(r_ref, source)
     left = left_side(newton_inverse(diag))
     for start, part in ((0, new_lower), (n, new_upper), (2 * n, source)):
         z = multiply(left, part)
@@ -189,9 +236,8 @@
     diag, source = load(diag_ref), load(rhs_ref)
     before, after = load(cl_ref), load(cr_ref)
     left_l, left_u = left_side(load(lower_ref)), left_side(load(upper_ref))
-    z = multiply(left_l, columns_of(before, n, None))
-    diag = minus(diag, columns_of(z, 0, n))
-    source = minus(source, columns_of(z, n, None))
+    diag = minus(diag, multiply(left_l, columns_of(before, n, 2 * n)))
+    source = minus(source, multiply(left_l, columns_of(before, 2 * n, None)))
     diag = minus(diag, multiply(left_u, columns_of(after, 0, n)))
     source = minus(source, multiply(left_u, columns_of(after, 2 * n, None)))
     left = [jnp.where(flag, u, l) for u, l in zip(left_u, left_l)]
@@ -209,10 +255,10 @@
 
 def last_kernel(diag_ref, rhs_ref, w_ref, coef_ref, out_ref):
     n = diag_ref.shape[1]
-    z = multiply(left_side(load(w_ref)), load(coef_ref))
+    z = wide_product(left_side(load(w_ref)), load(coef_ref))
+    source = minus(load(rhs_ref), columns_of(z, n, None))
     diag = minus(load(diag_ref), columns_of(z, 0, n))
-    source = minus(load(rhs_ref), columns_of(z, n, None))
-    save(out_ref, multiply(left_side(newton_inverse(diag)), source))
+    save(out_ref, newton_solve(diag, source))
 
 
 def run(kernel, out_shapes, args, products, scalars=0):
@@ -258,7 +304,7 @@
     pairs = jnp.concatenate([g_lesser[:, 0], g_greater[:, 0]], axis=0)
     pairs = pairs.reshape(4, energies, share, n).swapaxes(0, 1)
     pairs = lax.all_to_all(pairs, "energy", split_axis=0, concat_axis=0, tiled=True)
-    (polar,) = run(convolve_kernel, [(energies, 2, share, n)], [pairs], 0.02)
+    polar = convolve(pairs)
     core_flag, right_first, low_half = flag(first_core), flag(block & 2 == 0), flag(block < blocks // 2)
     polar, half_left, half_right, core_flag, right_first, low_half = lax.optimization_barrier(
         (polar, half_left, half_right, core_flag, right_first, low_half)
@@ -306,11 +352,18 @@
         2.5,
         1,
     )
-    diag, low, up, source, coef = run(
+    diag, mixed, source = run(
+        level1_middle_kernel,
+        [square, square, tall],
+        [right_first, diag, low, up, source, handed[0], handed[2]],
+        1.7,
+        1,
+    )
+    diag, low, up, coef = run(
         level1_kernel,
-        [square, square, square, tall, wide],
-        [right_first, diag, low, up, source, coupling, *handed],
-        7,
+        [square, square, square, wide],
+        [right_first, diag, low, up, source, coupling, mixed, handed[1]],
+        5.7,
         1,
     )
 

time: 199 us -> 196 us (0.985)
  waiting for transfers between devices: 118 us -> 116 us
  transfers between devices with their start and end apart: 19 -> 19, of which waited for: 11 -> 11; matrix products, arithmetic and copies ran while one was open for 0% -> 0% of each run, Pallas kernels for 1% -> 3%
where the time goes in v1:
time: 196 us
  waiting for transfers between devices  116 us (59%)
  starting transfers between devices  54.8 us (28%)
  Pallas kernels  19.4 us (10%)
  other arithmetic  3.12 us (2%)
  local copies, waits for them, and re-layouts  2.24 us (1%)
    ppermute x15, waiting for transfers between devices, send(): return lax.ppermute(value, 'block', pairs)  97.3 us
    ppermute x15, starting transfers between devices, send(): return lax.ppermute(value, 'block', pairs)  40.6 us
    all_to_all x1, waiting for transfers between devices, program(): lax.all_to_all(pairs, 'energy', split_axis=0, concat_axis=0, tiled=True)  18.4 us
    pallas_call x8, Pallas kernels, run(): pl.pallas_call(kernel, out_shape=outs, in_specs=specs, out_specs=[pl.Bloc...  17.9 us
    all_to_all x1, starting transfers between devices, program(): lax.all_to_all(pairs, 'energy', split_axis=0, concat_axis=0, tiled=True)  8.7 us
    all_to_all x1, starting transfers between devices, program(): lax.all_to_all(polar, 'energy', split_axis=0, concat_axis=0, tiled=True)  4.93 us
  transfers between devices with their start and end apart: 19, of which 11 were waited for; matrix products, arithmetic and copies ran while one was open for 0% of the time, Pallas kernels for 3%

profile of v1, /device:TPU:6, one launch (start us, length us, event | category | flops | bytes accessed | tf_op | source)
XLA Modules:
  0.0 195.6 jit_solution(1961850661339341141)
XLA Ops:
  0.0 2.3 %copy_bitcast_fusion = f32[16,4,16,256]{3,2,1,0:T(8,128)} fusion(f32[2,16,16,256]{3,2,1,0:T(8,128)} %bitcast.16, f32[2,16,16,256]{3,2,1,0:T(8,128)} %bitcast.17), kind=kLoop, calls=%fused_computation.1 | loop fusion | flops 262144 | bytes 2097152 | tf_op jit(solution)/shard_map/transpose | solution.py:305
  2.3 8.7 %all-to-all-start = ((f32[16,4,16,256]{3,2,1,0:T(8,128)}), f32[16,4,16,256]{3,2,1,0:T(8,128)S(1)}, u32[]{:S(2)}, u32[]{:S(2)}) async-start(f32[16,4,16,256]{3,2,1,0:T(8,128)} %copy_bitcast_fusion), calls=%async_computation | async-start | bytes 2097152 | tf_op jit(solution)/shard_map/all_to_all | solution.py:306
  11.9 5.2 %collective-permute-start.1 = (f32[2,256,256]{2,1,0:T(8,128)}, f32[2,256,256]{2,1,0:T(8,128)S(1)}, u32[]{:S(2)}, u32[]{:S(2)}) collective-permute-start(f32[2,256,256]{2,1,0:T(8,128)} %select_select_fusion), channel_id=1, source_target_pairs={{1,0},{2,1},{3,2},{4,3},{5,4},{6,5},{7,6},{8,7},{9,8},{10,9},{11,1... | collective-permute-start | bytes 1572872 | tf_op jit(solution)/shard_map/ppermute | solution.py:289
  19.0 18.4 %all-to-all-done.g_ref = f32[16,4,16,256]{3,2,1,0:T(8,128)S(1)} async-done(((f32[16,4,16,256]{3,2,1,0:T(8,128)}), f32[16,4,16,256]{3,2,1,0:T(8,128)S(1)}, u32[]{:S(2)}, u32[]{:S(2)}) %all-to-all-start) | async-done | bytes 1048608 | tf_op jit(solution)/shard_map/all_to_all | solution.py:306
  39.0 4.9 %all-to-all-start.1 = ((f32[16,2,16,256]{3,2,1,0:T(8,128)}), f32[16,2,16,256]{3,2,1,0:T(8,128)S(1)}, u32[]{:S(2)}, u32[]{:S(2)}) async-start(f32[16,2,16,256]{3,2,1,0:T(8,128)} %convolve.1), calls=%async_computation.1 | async-start | bytes 1048576 | tf_op jit(solution)/shard_map/all_to_all | solution.py:312
  44.6 5.2 %collective-permute-start.5 = (f32[2,256,128]{2,1,0:T(8,128)S(1)}, f32[2,256,128]{2,1,0:T(8,128)S(1)}, u32[]{:S(2)}, u32[]{:S(2)}) collective-permute-start(f32[2,256,128]{2,1,0:T(8,128)S(1)} %bitcast.13), channel_id=1, source_target_pairs={{1,0},{2,1},{3,2},{4,3},{5,4},{6,5},{7,6},{8,7},{9,8},{10,9},{11,1... | collective-permute-start | bytes 786440 | tf_op jit(solution)/shard_map/ppermute | solution.py:289
  51.7 4.2 %collective-permute-done.5.rr_ref = f32[2,256,128]{2,1,0:T(8,128)S(1)} collective-permute-done((f32[2,256,128]{2,1,0:T(8,128)S(1)}, f32[2,256,128]{2,1,0:T(8,128)S(1)}, u32[]{:S(2)}, u32[]{:S(2)}) %collective-permute-start.5) | collective-permute-done | bytes 262176 | tf_op jit(solution)/shard_map/ppermute | solution.py:289
  56.6 5.5 %collective-permute-done.4.rl_ref = f32[2,256,128]{2,1,0:T(8,128)S(1)} collective-permute-done((f32[2,256,128]{2,1,0:T(8,128)S(1)}, f32[2,256,128]{2,1,0:T(8,128)S(1)}, u32[]{:S(2)}, u32[]{:S(2)}) %collective-permute-start.4) | collective-permute-done | bytes 262176 | tf_op jit(solution)/shard_map/ppermute | solution.py:289
  66.5 3.9 %collective-permute-start.6 = (f32[2,256,256]{2,1,0:T(8,128)S(1)}, f32[2,256,256]{2,1,0:T(8,128)S(1)}, u32[]{:S(2)}, u32[]{:S(2)}) collective-permute-start(f32[2,256,256]{2,1,0:T(8,128)S(1)} %get-tuple-element.50), channel_id=1, source_target_pairs={{0,1},{1,2},{2,3},{3,4},{4,5},{5,6},{6,7},{7,8},{8,9},{9,10},{10,1... | collective-permute-start | bytes 1572872 | tf_op jit(solution)/shard_map/ppermute | solution.py:289
  70.5 9.1 %collective-permute-done.7.xr_ref = f32[2,256,256]{2,1,0:T(8,128)S(1)} collective-permute-done((f32[2,256,256]{2,1,0:T(8,128)S(1)}, f32[2,256,256]{2,1,0:T(8,128)S(1)}, u32[]{:S(2)}, u32[]{:S(2)}) %collective-permute-start.7) | collective-permute-done | bytes 524320 | tf_op jit(solution)/shard_map/ppermute | solution.py:289
  79.6 5.7 %collective-permute-done.6.xl_ref = f32[2,256,256]{2,1,0:T(8,128)S(1)} collective-permute-done((f32[2,256,256]{2,1,0:T(8,128)S(1)}, f32[2,256,256]{2,1,0:T(8,128)S(1)}, u32[]{:S(2)}, u32[]{:S(2)}) %collective-permute-start.6) | collective-permute-done | bytes 524320 | tf_op jit(solution)/shard_map/ppermute | solution.py:289
  85.3 4.5 %shard_map.65 = (f32[2,256,256]{2,1,0:T(8,128)S(1)}, f32[2,256,256]{2,1,0:T(8,128)S(1)}, f32[2,256,256]{2,1,0:T(8,128)S(1)}, f32[2,256,256]{2,1,0:T(8,128)S(1)},...) custom-call(s32[1]{0:T(128)} %bitcast.3.core_ref, f32[2,256,256]{2,1,0:T(8,128)S(1)} %get-tuple-element.49.diag_ref, ...), custom_call_target="tpu_custom_call" | custom-call | flops 3221225472 | bytes 7864324 | tf_op jit(solution)/shard_map/pallas_call | solution.py:269
  91.8 3.6 %collective-permute-start.9 = (f32[2,256,256]{2,1,0:T(8,128)S(1)}, f32[2,256,256]{2,1,0:T(8,128)S(1)}, u32[]{:S(2)}, u32[]{:S(2)}) collective-permute-start(f32[2,256,256]{2,1,0:T(8,128)S(1)} %get-tuple-element.63), channel_id=1, source_target_pairs={{0,2},{1,3},{2,0},{3,1},{4,6},{5,7},{6,4},{7,5},{8,10},{9,11},{10,... | collective-permute-start | bytes 1572872 | tf_op jit(solution)/shard_map/ppermute | solution.py:289
  95.4 10.8 %collective-permute-done.8.pa_ref = f32[2,256,256]{2,1,0:T(8,128)S(1)} collective-permute-done((f32[2,256,256]{2,1,0:T(8,128)S(1)}, f32[2,256,256]{2,1,0:T(8,128)S(1)}, u32[]{:S(2)}, u32[]{:S(2)}) %collective-permute-start.8) | collective-permute-done | bytes 524320 | tf_op jit(solution)/shard_map/ppermute | solution.py:289
  107.5 9.0 %collective-permute-done.9.pb_ref = f32[2,256,256]{2,1,0:T(8,128)S(1)} collective-permute-done((f32[2,256,256]{2,1,0:T(8,128)S(1)}, f32[2,256,256]{2,1,0:T(8,128)S(1)}, u32[]{:S(2)}, u32[]{:S(2)}) %collective-permute-start.9) | collective-permute-done | bytes 524320 | tf_op jit(solution)/shard_map/ppermute | solution.py:289
  119.4 6.2 %collective-permute-start.12 = (f32[2,256,128]{2,1,0:T(8,128)S(1)}, f32[2,256,128]{2,1,0:T(8,128)S(1)}, u32[]{:S(2)}, u32[]{:S(2)}) collective-permute-start(f32[2,256,128]{2,1,0:T(8,128)S(1)} %get-tuple-element.64), channel_id=1, source_target_pairs={{2,4},{3,5},{4,2},{5,3},{6,8},{7,9},{8,6},{9,7},{10,12},{11,13},{1... | collective-permute-start | bytes 786440 | tf_op jit(solution)/shard_map/ppermute | solution.py:289
  125.6 6.8 %collective-permute-done.10.pr_ref = f32[2,256,128]{2,1,0:T(8,128)S(1)} collective-permute-done((f32[2,256,128]{2,1,0:T(8,128)S(1)}, f32[2,256,128]{2,1,0:T(8,128)S(1)}, u32[]{:S(2)}, u32[]{:S(2)}) %collective-permute-start.10) | collective-permute-done | bytes 262176 | tf_op jit(solution)/shard_map/ppermute | solution.py:289
  134.4 2.6 %shard_map.69 = (f32[2,256,256]{2,1,0:T(8,128)S(1)}, f32[2,256,256]{2,1,0:T(8,128)S(1)}, f32[2,256,256]{2,1,0:T(8,128)S(1)}, f32[2,256,640]{2,1,0:T(8,128)S(1)}) custom-call(s32[1]{0:T(128)} %bitcast.4.flag_ref, f32[2,256,256]{2,1,0:T(8,128)S(1)} %get-tuple-element.67.diag_ref, f32[2,256,256]{2,1,0:T(8,128)S(1)} %get-tuple-element.54.lower_ref, ...), custom_call_target="tpu_custom_call" | custom-call | flops 2295123200 | bytes 6291460 | tf_op jit(solution)/shard_map/pallas_call | solution.py:269
  136.9 4.3 %collective-permute-start.15 = (f32[2,256,640]{2,1,0:T(8,128)S(1)}, f32[2,256,640]{2,1,0:T(8,128)S(1)}, u32[]{:S(2)}, u32[]{:S(2)}) collective-permute-start(f32[2,256,640]{2,1,0:T(8,128)S(1)} %get-tuple-element.74), channel_id=1, source_target_pairs={{4,0},{5,1},{6,2},{7,3},{8,4},{9,5},{10,6},{11,7},{12,8},{13,9},{1... | collective-permute-start | bytes 3932168 | tf_op jit(solution)/shard_map/ppermute | solution.py:289
  142.6 24.8 %collective-permute-done.15.cr_ref = f32[2,256,640]{2,1,0:T(8,128)S(1)} collective-permute-done((f32[2,256,640]{2,1,0:T(8,128)S(1)}, f32[2,256,640]{2,1,0:T(8,128)S(1)}, u32[]{:S(2)}, u32[]{:S(2)}) %collective-permute-start.15) | collective-permute-done | bytes 1310752 | tf_op jit(solution)/shard_map/ppermute | solution.py:289
  167.4 4.2 %collective-permute-done.14.cl_ref = f32[2,256,640]{2,1,0:T(8,128)S(1)} collective-permute-done((f32[2,256,640]{2,1,0:T(8,128)S(1)}, f32[2,256,640]{2,1,0:T(8,128)S(1)}, u32[]{:S(2)}, u32[]{:S(2)}) %collective-permute-start.14) | collective-permute-done | bytes 1310752 | tf_op jit(solution)/shard_map/ppermute | solution.py:289
  171.6 3.4 %shard_map.70 = (f32[2,256,256]{2,1,0:T(8,128)S(1)}, f32[2,256,128]{2,1,0:T(8,128)S(1)}, f32[2,256,256]{2,1,0:T(8,128)S(1)}, f32[2,256,384]{2,1,0:T(8,128)S(1)}) custom-call(s32[1]{0:T(128)} %bitcast.5.flag_ref, f32[2,256,256]{2,1,0:T(8,128)S(1)} %get-tuple-element.71.diag_ref, f32[2,256,256]{2,1,0:T(8,128)S(1)} %get-tuple-element.72.lower_ref, ...), custom_call_target="tpu_custom_call" | custom-call | flops 3019898880 | bytes 6553604 | tf_op jit(solution)/shard_map/pallas_call | solution.py:269
  175.9 17.1 %collective-permute-done.16.coef_ref = f32[2,256,384]{2,1,0:T(8,128)S(1)} collective-permute-done((f32[2,256,384]{2,1,0:T(8,128)S(1)}, f32[2,256,384]{2,1,0:T(8,128)S(1)}, u32[]{:S(2)}, u32[]{:S(2)}) %collective-permute-start.16) | collective-permute-done | bytes 786464 | tf_op jit(solution)/shard_map/ppermute | solution.py:289
  193.0 2.7 %shard_map.71 = f32[2,256,128]{2,1,0:T(8,128)} custom-call(f32[2,256,256]{2,1,0:T(8,128)S(1)} %get-tuple-element.75.diag_ref, f32[2,256,128]{2,1,0:T(8,128)S(1)} %get-tuple-element.76.rhs_ref, f32[2,256,256]{2,1,0:T(8,128)S(1)} %get-tuple-element.77.w_ref, f32[2,256,384]{2,1,0:T(8,128)S(1)} %collective-permute-done.16.coef_ref), custom_call_target="tpu_custom_call" | custom-call | flops 1610612736 | bytes 2359296 | tf_op jit(solution)/shard_map/pallas_call | solution.py:269
  (45 shorter events, 22.1 us)
Async XLA Ops:
  2.3 8.7 %copy-start = (f32[2,256,256]{2,1,0:T(8,128)S(1)}, f32[2,256,256]{2,1,0:T(8,128)}, u32[]{:S(2)}) copy-start(f32[2,256,256]{2,1,0:T(8,128)} %lower_ref.1) | copy-start | bytes 1572868
  2.3 8.7 %copy-start.1 = (f32[2,256,256]{2,1,0:T(8,128)S(1)}, f32[2,256,256]{2,1,0:T(8,128)}, u32[]{:S(2)}) copy-start(f32[2,256,256]{2,1,0:T(8,128)} %upper_ref.1) | copy-start | bytes 1572868
  2.3 35.2 %all-to-all-start = ((f32[16,4,16,256]{3,2,1,0:T(8,128)}), f32[16,4,16,256]{3,2,1,0:T(8,128)S(1)}, u32[]{:S(2)}, u32[]{:S(2)}) async-start(f32[16,4,16,256]{3,2,1,0:T(8,128)} %copy_bitcast_fusion), calls=%async_computation | async-start | bytes 2097152 | tf_op jit(solution)/shard_map/all_to_all | solution.py:306
  11.9 27.1 %collective-permute-start.1 = (f32[2,256,256]{2,1,0:T(8,128)}, f32[2,256,256]{2,1,0:T(8,128)S(1)}, u32[]{:S(2)}, u32[]{:S(2)}) collective-permute-start(f32[2,256,256]{2,1,0:T(8,128)} %select_select_fusion), channel_id=1, source_target_pairs={{1,0},{2,1},{3,2},{4,3},{5,4},{6,5},{7,6},{8,7},{9,8},{10,9},{11,1... | collective-permute-start | bytes 1572872 | tf_op jit(solution)/shard_map/ppermute | solution.py:289
  17.1 21.9 %collective-permute-start = (f32[2,256,256]{2,1,0:T(8,128)}, f32[2,256,256]{2,1,0:T(8,128)}, u32[]{:S(2)}, u32[]{:S(2)}) collective-permute-start(f32[2,256,256]{2,1,0:T(8,128)} %select_select_fusion), channel_id=1, source_target_pairs={{0,1},{1,2},{2,3},{3,4},{4,5},{5,6},{6,7},{7,8},{8,9},{9,10},{10,1... | collective-permute-start | bytes 1572872 | tf_op jit(solution)/shard_map/ppermute | solution.py:289
  19.0 25.6 %copy-start.5 = (f32[2,1,256,128]{3,2,1,0:T(8,128)S(1)}, f32[2,1,256,128]{3,2,1,0:T(8,128)}, u32[]{:S(2)}) copy-start(f32[2,1,256,128]{3,2,1,0:T(8,128)} %param.11) | copy-start | bytes 786436
  19.0 44.6 %copy-start.2 = (f32[2,1,256,256]{3,2,1,0:T(8,128)S(1)}, f32[2,1,256,256]{3,2,1,0:T(8,128)}, u32[]{:S(2)}) copy-start(f32[2,1,256,256]{3,2,1,0:T(8,128)} %param.8) | copy-start | bytes 1572868
  39.0 24.6 %all-to-all-start.1 = ((f32[16,2,16,256]{3,2,1,0:T(8,128)}), f32[16,2,16,256]{3,2,1,0:T(8,128)S(1)}, u32[]{:S(2)}, u32[]{:S(2)}) async-start(f32[16,2,16,256]{3,2,1,0:T(8,128)} %convolve.1), calls=%async_computation.1 | async-start | bytes 1048576 | tf_op jit(solution)/shard_map/all_to_all | solution.py:312
  43.9 18.9 %collective-permute-start.2 = (f32[2,256,256]{2,1,0:T(8,128)}, f32[2,256,256]{2,1,0:T(8,128)S(1)}, u32[]{:S(2)}, u32[]{:S(2)}) collective-permute-start(f32[2,256,256]{2,1,0:T(8,128)} %collective-permute-done.hl_ref), channel_id=1, source_target_pairs={{0,16},{16,0},{32,48},{48,32},{64,80},{80,64},{96,112},{112,96},{1... | collective-permute-start | bytes 1572872 | tf_op jit(solution)/shard_map/ppermute | solution.py:314
  44.5 19.1 %collective-permute-start.3 = (f32[2,256,256]{2,1,0:T(8,128)S(1)}, f32[2,256,256]{2,1,0:T(8,128)S(1)}, u32[]{:S(2)}, u32[]{:S(2)}) collective-permute-start(f32[2,256,256]{2,1,0:T(8,128)S(1)} %collective-permute-done.1.hr_ref), channel_id=1, source_target_pairs={{0,16},{16,0},{32,48},{48,32},{64,80},{80,64},{96,112},{112,96},{1... | collective-permute-start | bytes 1572872 | tf_op jit(solution)/shard_map/ppermute | solution.py:315
  44.6 11.3 %collective-permute-start.5 = (f32[2,256,128]{2,1,0:T(8,128)S(1)}, f32[2,256,128]{2,1,0:T(8,128)S(1)}, u32[]{:S(2)}, u32[]{:S(2)}) collective-permute-start(f32[2,256,128]{2,1,0:T(8,128)S(1)} %bitcast.13), channel_id=1, source_target_pairs={{1,0},{2,1},{3,2},{4,3},{5,4},{6,5},{7,6},{8,7},{9,8},{10,9},{11,1... | collective-permute-start | bytes 786440 | tf_op jit(solution)/shard_map/ppermute | solution.py:289
  49.7 12.3 %collective-permute-start.4 = (f32[2,256,128]{2,1,0:T(8,128)S(1)}, f32[2,256,128]{2,1,0:T(8,128)S(1)}, u32[]{:S(2)}, u32[]{:S(2)}) collective-permute-start(f32[2,256,128]{2,1,0:T(8,128)S(1)} %bitcast.14), channel_id=1, source_target_pairs={{0,1},{1,2},{2,3},{3,4},{4,5},{5,6},{6,7},{7,8},{8,9},{9,10},{10,1... | collective-permute-start | bytes 786440 | tf_op jit(solution)/shard_map/ppermute | solution.py:289
  63.6 21.7 %copy-start.4 = (f32[2,256,256]{2,1,0:T(8,128)S(1)}, f32[2,256,256]{2,1,0:T(8,128)}, u32[]{:S(2)}) copy-start(f32[2,256,256]{2,1,0:T(8,128)} %copy-done.3) | copy-start | bytes 1572868
  64.6 15.0 %collective-permute-start.7 = (f32[2,256,256]{2,1,0:T(8,128)S(1)}, f32[2,256,256]{2,1,0:T(8,128)S(1)}, u32[]{:S(2)}, u32[]{:S(2)}) collective-permute-start(f32[2,256,256]{2,1,0:T(8,128)S(1)} %get-tuple-element.50), channel_id=1, source_target_pairs={{1,0},{2,1},{3,2},{4,3},{5,4},{6,5},{7,6},{8,7},{9,8},{10,9},{11,1... | collective-permute-start | bytes 1572872 | tf_op jit(solution)/shard_map/ppermute | solution.py:289
  66.5 18.7 %collective-permute-start.6 = (f32[2,256,256]{2,1,0:T(8,128)S(1)}, f32[2,256,256]{2,1,0:T(8,128)S(1)}, u32[]{:S(2)}, u32[]{:S(2)}) collective-permute-start(f32[2,256,256]{2,1,0:T(8,128)S(1)} %get-tuple-element.50), channel_id=1, source_target_pairs={{0,1},{1,2},{2,3},{3,4},{4,5},{5,6},{6,7},{7,8},{8,9},{9,10},{10,1... | collective-permute-start | bytes 1572872 | tf_op jit(solution)/shard_map/ppermute | solution.py:289
  89.8 16.4 %collective-permute-start.8 = (f32[2,256,256]{2,1,0:T(8,128)S(1)}, f32[2,256,256]{2,1,0:T(8,128)S(1)}, u32[]{:S(2)}, u32[]{:S(2)}) collective-permute-start(f32[2,256,256]{2,1,0:T(8,128)S(1)} %get-tuple-element.62), channel_id=1, source_target_pairs={{0,2},{1,3},{2,0},{3,1},{4,6},{5,7},{6,4},{7,5},{8,10},{9,11},{10,... | collective-permute-start | bytes 1572872 | tf_op jit(solution)/shard_map/ppermute | solution.py:289
  91.8 24.7 %collective-permute-start.9 = (f32[2,256,256]{2,1,0:T(8,128)S(1)}, f32[2,256,256]{2,1,0:T(8,128)S(1)}, u32[]{:S(2)}, u32[]{:S(2)}) collective-permute-start(f32[2,256,256]{2,1,0:T(8,128)S(1)} %get-tuple-element.63), channel_id=1, source_target_pairs={{0,2},{1,3},{2,0},{3,1},{4,6},{5,7},{6,4},{7,5},{8,10},{9,11},{10,... | collective-permute-start | bytes 1572872 | tf_op jit(solution)/shard_map/ppermute | solution.py:289
  106.2 27.3 %collective-permute-start.11 = (f32[2,256,256]{2,1,0:T(8,128)S(1)}, f32[2,256,256]{2,1,0:T(8,128)S(1)}, u32[]{:S(2)}, u32[]{:S(2)}) collective-permute-start(f32[2,256,256]{2,1,0:T(8,128)S(1)} %collective-permute-done.8.pa_ref), channel_id=1, source_target_pairs={{0,4},{1,5},{4,8},{5,9},{6,2},{7,3},{8,12},{9,13},{10,6},{11,7},{1... | collective-permute-start | bytes 1572872 | tf_op jit(solution)/shard_map/ppermute | solution.py:289
  116.5 17.8 %collective-permute-start.13 = (f32[2,256,256]{2,1,0:T(8,128)S(1)}, f32[2,256,256]{2,1,0:T(8,128)S(1)}, u32[]{:S(2)}, u32[]{:S(2)}) collective-permute-start(f32[2,256,256]{2,1,0:T(8,128)S(1)} %collective-permute-done.9.pb_ref), channel_id=1, source_target_pairs={{0,4},{1,5},{4,8},{5,9},{6,2},{7,3},{8,12},{9,13},{10,6},{11,7},{1... | collective-permute-start | bytes 1572872 | tf_op jit(solution)/shard_map/ppermute | solution.py:289
  117.8 14.6 %collective-permute-start.10 = (f32[2,256,128]{2,1,0:T(8,128)S(1)}, f32[2,256,128]{2,1,0:T(8,128)S(1)}, u32[]{:S(2)}, u32[]{:S(2)}) collective-permute-start(f32[2,256,128]{2,1,0:T(8,128)S(1)} %get-tuple-element.64), channel_id=1, source_target_pairs={{0,2},{1,3},{2,0},{3,1},{4,6},{5,7},{6,4},{7,5},{8,10},{9,11},{10,... | collective-permute-start | bytes 786440 | tf_op jit(solution)/shard_map/ppermute | solution.py:289
  119.4 14.2 %collective-permute-start.12 = (f32[2,256,128]{2,1,0:T(8,128)S(1)}, f32[2,256,128]{2,1,0:T(8,128)S(1)}, u32[]{:S(2)}, u32[]{:S(2)}) collective-permute-start(f32[2,256,128]{2,1,0:T(8,128)S(1)} %get-tuple-element.64), channel_id=1, source_target_pairs={{2,4},{3,5},{4,2},{5,3},{6,8},{7,9},{8,6},{9,7},{10,12},{11,13},{1... | collective-permute-start | bytes 786440 | tf_op jit(solution)/shard_map/ppermute | solution.py:289
  136.9 30.5 %collective-permute-start.15 = (f32[2,256,640]{2,1,0:T(8,128)S(1)}, f32[2,256,640]{2,1,0:T(8,128)S(1)}, u32[]{:S(2)}, u32[]{:S(2)}) collective-permute-start(f32[2,256,640]{2,1,0:T(8,128)S(1)} %get-tuple-element.74), channel_id=1, source_target_pairs={{4,0},{5,1},{6,2},{7,3},{8,4},{9,5},{10,6},{11,7},{12,8},{13,9},{1... | collective-permute-start | bytes 3932168 | tf_op jit(solution)/shard_map/ppermute | solution.py:289
  141.3 30.3 %collective-permute-start.14 = (f32[2,256,640]{2,1,0:T(8,128)S(1)}, f32[2,256,640]{2,1,0:T(8,128)S(1)}, u32[]{:S(2)}, u32[]{:S(2)}) collective-permute-start(f32[2,256,640]{2,1,0:T(8,128)S(1)} %get-tuple-element.74), channel_id=1, source_target_pairs={{0,4},{1,5},{2,6},{3,7},{4,8},{5,9},{6,10},{7,11},{8,12},{9,13},{1... | collective-permute-start | bytes 3932168 | tf_op jit(solution)/shard_map/ppermute | solution.py:289
  175.0 17.9 %collective-permute-start.16 = (f32[2,256,384]{2,1,0:T(8,128)S(1)}, f32[2,256,384]{2,1,0:T(8,128)S(1)}, u32[]{:S(2)}, u32[]{:S(2)}) collective-permute-start(f32[2,256,384]{2,1,0:T(8,128)S(1)} %get-tuple-element.78), channel_id=1, source_target_pairs={{0,8},{1,9},{2,10},{3,11},{4,12},{5,13},{6,14},{7,15},{8,0},{9,1},... | collective-permute-start | bytes 2359304 | tf_op jit(solution)/shard_map/ppermute | solution.py:289
  (5 other events, 11.5 us)

commit v2 on v1

--- a/solution.py
+++ b/solution.py
@@ -143,22 +143,26 @@
     save(inverse_ref, newton_inverse(diag))
 
 
+def level0_after_kernel(core_ref, diag_ref, upper_ref, xr_ref, hr_ref, or_ref, d_ref, tr_ref):
+    flag = core_ref[0] > 0
+    after = multiply(left_side(load(upper_ref)), load(xr_ref))
+    save(tr_ref, after)
+    z = multiply(left_side(after), choose(flag, load(hr_ref), load(or_ref)))
+    save(d_ref, minus(load(diag_ref), z))
+
+
 def level0_kernel(
-    core_ref, diag_ref, lower_ref, upper_ref, xl_ref, xr_ref, hl_ref, ol_ref, hr_ref, or_ref,
-    d_ref, l_ref, alpha_ref, inverse_ref, tl_ref, tr_ref,
+    core_ref, diag_ref, lower_ref, xl_ref, hl_ref, ol_ref,
+    d_ref, l_ref, alpha_ref, inverse_ref, tl_ref,
 ):
     flag = core_ref[0] > 0
-    diag = load(diag_ref)
     before = multiply(left_side(load(lower_ref)), load(xl_ref))
     save(tl_ref, before)
     left = left_side(before)
     zh, zo = multiply(left, load(hl_ref)), multiply(left, load(ol_ref))
-    diag = minus(diag, choose(flag, zo, zh))
+    diag = minus(load(diag_ref), choose(flag, zo, zh))
     new_lower = negative(choose(flag, zh, zo))
     save(l_ref, new_lower)
-    after = multiply(left_side(load(upper_ref)), load(xr_ref))
-    save(tr_ref, after)
-    diag = minus(diag, multiply(left_side(after), choose(flag, load(hr_ref), load(or_ref))))
     save(d_ref, diag)
     inverse = newton_inverse(diag)
     save(inverse_ref, inverse)
@@ -227,22 +231,24 @@
         coef_ref[1, :, start : start + part[0].shape[1]] = z[1]
 
 
+def level2_after_kernel(diag_ref, upper_ref, rhs_ref, cr_ref, d_ref, r_ref, z_ref):
+    n = diag_ref.shape[1]
+    after, left = load(cr_ref), left_side(load(upper_ref))
+    save(d_ref, minus(load(diag_ref), multiply(left, columns_of(after, 0, n))))
+    save(r_ref, minus(load(rhs_ref), multiply(left, columns_of(after, 2 * n, None))))
+    save(z_ref, multiply(left, columns_of(after, n, 2 * n)))
+
+
 def level2_kernel(
-    flag_ref, diag_ref, lower_ref, upper_ref, rhs_ref, cl_ref, cr_ref,
+    flag_ref, diag_ref, lower_ref, rhs_ref, z_ref, cl_ref,
     d_ref, r_ref, w_ref, coef_ref,
 ):
     flag = flag_ref[0] > 0
     n = diag_ref.shape[1]
-    diag, source = load(diag_ref), load(rhs_ref)
-    before, after = load(cl_ref), load(cr_ref)
-    left_l, left_u = left_side(load(lower_ref)), left_side(load(upper_ref))
-    diag = minus(diag, multiply(left_l, columns_of(before, n, 2 * n)))
-    source = minus(source, multiply(left_l, columns_of(before, 2 * n, None)))
-    diag = minus(diag, multiply(left_u, columns_of(after, 0, n)))
-    source = minus(source, multiply(left_u, columns_of(after, 2 * n, None)))
-    left = [jnp.where(flag, u, l) for u, l in zip(left_u, left_l)]
-    other = choose(flag, columns_of(after, n, 2 * n), columns_of(before, 0, n))
-    coupling = negative(multiply(left, other))
+    before, left = load(cl_ref), left_side(load(lower_ref))
+    diag = minus(load(diag_ref), multiply(left, columns_of(before, n, 2 * n)))
+    source = minus(load(rhs_ref), multiply(left, columns_of(before, 2 * n, None)))
+    coupling = negative(choose(flag, load(z_ref), multiply(left, columns_of(before, 0, n))))
     save(d_ref, diag)
     save(r_ref, source)
     save(w_ref, coupling)
@@ -321,12 +327,20 @@
     square, wide = (2, n, n), (2, n, 2 * n + columns)
     slim, tall = (2, n, n + columns), (2, n, columns)
     diag, inverse = run(first_kernel, [square, square], [onsite, polar], 2)
-    inverse_left, inverse_right = shift(inverse, 1), shift(inverse, -1)
-    diag, low, alpha, inverse, through_left, through_right = run(
+    inverse_right = shift(inverse, -1)
+    inverse_left = shift(inverse, 1)
+    diag, through_right = run(
+        level0_after_kernel,
+        [square] * 2,
+        [core_flag, diag, upper, inverse_right, half_right, other_right],
+        2,
+        1,
+    )
+    diag, low, alpha, inverse, through_left = run(
         level0_kernel,
-        [square] * 6,
-        [core_flag, diag, lower, upper, inverse_left, inverse_right, half_left, other_left, half_right, other_right],
-        8,
+        [square] * 5,
+        [core_flag, diag, lower, inverse_left, half_left, other_left],
+        6,
         1,
     )
     up, source, beta, rho = run(
@@ -367,12 +381,16 @@
         1,
     )
 
-    coef_left, coef_right = shift(coef, 4), shift(coef, -4)
+    coef_right = shift(coef, -4)
+    coef_left = shift(coef, 4)
+    diag, source, mixed = run(
+        level2_after_kernel, [square, tall, square], [diag, up, source, coef_right], 2.5
+    )
     diag, source, coupling, coef = run(
         level2_kernel,
         [square, tall, square, slim],
-        [low_half, diag, low, up, source, coef_left, coef_right],
-        7.5,
+        [low_half, diag, low, source, mixed, coef_left],
+        6,
         1,
     )
     coef = send(coef, [(b, b ^ 8) for b in range(blocks)])

time: 196 us -> 195 us (level)
  waiting for transfers between devices: 116 us -> 114 us
    ppermute x15, waiting for transfers between devices: 97.3 us -> 95.3 us  [send(): return lax.ppermute(value, 'block', pairs)]
    pallas_call x8 -> x10, Pallas kernels: 17.9 us -> 18.7 us  [run(): pl.pallas_call(kernel, out_shape=outs, in_specs=specs, out_specs=[pl.Bloc...]
  transfers between devices with their start and end apart: 19 -> 19, of which waited for: 11 -> 11; matrix products, arithmetic and copies ran while one was open for 0% -> 0% of each run, Pallas kernels for 3% -> 4%
where the time goes in v2:
time: 195 us; the launch traced here: 194 us
  waiting for transfers between devices  114 us (58%)
  starting transfers between devices  54.8 us (28%)
  Pallas kernels  20.2 us (10%)
  other arithmetic  3.14 us (2%)
  local copies, waits for them, and re-layouts  2.24 us (1%)
    ppermute x15, waiting for transfers between devices, send(): return lax.ppermute(value, 'block', pairs)  95.3 us
    ppermute x15, starting transfers between devices, send(): return lax.ppermute(value, 'block', pairs)  40.5 us
    pallas_call x10, Pallas kernels, run(): pl.pallas_call(kernel, out_shape=outs, in_specs=specs, out_specs=[pl.Bloc...  18.7 us
    all_to_all x1, waiting for transfers between devices, program(): lax.all_to_all(pairs, 'energy', split_axis=0, concat_axis=0, tiled=True)  18.4 us
    all_to_all x1, starting transfers between devices, program(): lax.all_to_all(pairs, 'energy', split_axis=0, concat_axis=0, tiled=True)  8.7 us
    all_to_all x1, starting transfers between devices, program(): lax.all_to_all(polar, 'energy', split_axis=0, concat_axis=0, tiled=True)  4.93 us
  transfers between devices with their start and end apart: 19, of which 11 were waited for; matrix products, arithmetic and copies ran while one was open for 0% of the time, Pallas kernels for 4%

profile of v2, /device:TPU:6, one launch (start us, length us, event | category | flops | bytes accessed | tf_op | source)
XLA Modules:
  0.0 194.4 jit_solution(13582331719620194968)
XLA Ops:
  0.0 2.3 %copy_bitcast_fusion = f32[16,4,16,256]{3,2,1,0:T(8,128)} fusion(f32[2,16,16,256]{3,2,1,0:T(8,128)} %bitcast.16, f32[2,16,16,256]{3,2,1,0:T(8,128)} %bitcast.17), kind=kLoop, calls=%fused_computation.1 | loop fusion | flops 262144 | bytes 2097152 | tf_op jit(solution)/shard_map/transpose | solution.py:311
  2.3 8.7 %all-to-all-start = ((f32[16,4,16,256]{3,2,1,0:T(8,128)}), f32[16,4,16,256]{3,2,1,0:T(8,128)S(1)}, u32[]{:S(2)}, u32[]{:S(2)}) async-start(f32[16,4,16,256]{3,2,1,0:T(8,128)} %copy_bitcast_fusion), calls=%async_computation | async-start | bytes 2097152 | tf_op jit(solution)/shard_map/all_to_all | solution.py:312
  11.9 5.2 %collective-permute-start.1 = (f32[2,256,256]{2,1,0:T(8,128)}, f32[2,256,256]{2,1,0:T(8,128)S(1)}, u32[]{:S(2)}, u32[]{:S(2)}) collective-permute-start(f32[2,256,256]{2,1,0:T(8,128)} %select_select_fusion), channel_id=1, source_target_pairs={{1,0},{2,1},{3,2},{4,3},{5,4},{6,5},{7,6},{8,7},{9,8},{10,9},{11,1... | collective-permute-start | bytes 1572872 | tf_op jit(solution)/shard_map/ppermute | solution.py:295
  19.0 18.4 %all-to-all-done.g_ref = f32[16,4,16,256]{3,2,1,0:T(8,128)S(1)} async-done(((f32[16,4,16,256]{3,2,1,0:T(8,128)}), f32[16,4,16,256]{3,2,1,0:T(8,128)S(1)}, u32[]{:S(2)}, u32[]{:S(2)}) %all-to-all-start) | async-done | bytes 1048608 | tf_op jit(solution)/shard_map/all_to_all | solution.py:312
  39.0 4.9 %all-to-all-start.1 = ((f32[16,2,16,256]{3,2,1,0:T(8,128)}), f32[16,2,16,256]{3,2,1,0:T(8,128)S(1)}, u32[]{:S(2)}, u32[]{:S(2)}) async-start(f32[16,2,16,256]{3,2,1,0:T(8,128)} %convolve.1), calls=%async_computation.1 | async-start | bytes 1048576 | tf_op jit(solution)/shard_map/all_to_all | solution.py:318
  44.6 5.2 %collective-permute-start.5 = (f32[2,256,128]{2,1,0:T(8,128)S(1)}, f32[2,256,128]{2,1,0:T(8,128)S(1)}, u32[]{:S(2)}, u32[]{:S(2)}) collective-permute-start(f32[2,256,128]{2,1,0:T(8,128)S(1)} %bitcast.13), channel_id=1, source_target_pairs={{1,0},{2,1},{3,2},{4,3},{5,4},{6,5},{7,6},{8,7},{9,8},{10,9},{11,1... | collective-permute-start | bytes 786440 | tf_op jit(solution)/shard_map/ppermute | solution.py:295
  51.7 4.2 %collective-permute-done.5.rr_ref = f32[2,256,128]{2,1,0:T(8,128)S(1)} collective-permute-done((f32[2,256,128]{2,1,0:T(8,128)S(1)}, f32[2,256,128]{2,1,0:T(8,128)S(1)}, u32[]{:S(2)}, u32[]{:S(2)}) %collective-permute-start.5) | collective-permute-done | bytes 262176 | tf_op jit(solution)/shard_map/ppermute | solution.py:295
  56.6 5.5 %collective-permute-done.4.rl_ref = f32[2,256,128]{2,1,0:T(8,128)S(1)} collective-permute-done((f32[2,256,128]{2,1,0:T(8,128)S(1)}, f32[2,256,128]{2,1,0:T(8,128)S(1)}, u32[]{:S(2)}, u32[]{:S(2)}) %collective-permute-start.4) | collective-permute-done | bytes 262176 | tf_op jit(solution)/shard_map/ppermute | solution.py:295
  66.6 3.9 %collective-permute-start.7 = (f32[2,256,256]{2,1,0:T(8,128)S(1)}, f32[2,256,256]{2,1,0:T(8,128)S(1)}, u32[]{:S(2)}, u32[]{:S(2)}) collective-permute-start(f32[2,256,256]{2,1,0:T(8,128)S(1)} %get-tuple-element.54), channel_id=1, source_target_pairs={{0,1},{1,2},{2,3},{3,4},{4,5},{5,6},{6,7},{7,8},{8,9},{9,10},{10,1... | collective-permute-start | bytes 1572872 | tf_op jit(solution)/shard_map/ppermute | solution.py:295
  70.5 9.1 %collective-permute-done.6.xr_ref = f32[2,256,256]{2,1,0:T(8,128)S(1)} collective-permute-done((f32[2,256,256]{2,1,0:T(8,128)S(1)}, f32[2,256,256]{2,1,0:T(8,128)S(1)}, u32[]{:S(2)}, u32[]{:S(2)}) %collective-permute-start.6) | collective-permute-done | bytes 524320 | tf_op jit(solution)/shard_map/ppermute | solution.py:295
  80.6 4.7 %collective-permute-done.7.xl_ref = f32[2,256,256]{2,1,0:T(8,128)S(1)} collective-permute-done((f32[2,256,256]{2,1,0:T(8,128)S(1)}, f32[2,256,256]{2,1,0:T(8,128)S(1)}, u32[]{:S(2)}, u32[]{:S(2)}) %collective-permute-start.7) | collective-permute-done | bytes 524320 | tf_op jit(solution)/shard_map/ppermute | solution.py:295
  85.3 3.8 %shard_map.66 = (f32[2,256,256]{2,1,0:T(8,128)S(1)}, f32[2,256,256]{2,1,0:T(8,128)S(1)}, f32[2,256,256]{2,1,0:T(8,128)S(1)}, f32[2,256,256]{2,1,0:T(8,128)S(1)}, f32[2,256,256]{2,1,0:T(8,128)S(1)}) custom-call(s32[1]{0:T(128)} %bitcast.3.core_ref, f32[2,256,256]{2,1,0:T(8,128)S(1)} %get-tuple-element.56.diag_ref, f32[2,256,256]{2,1,0:T(8,128)S(1)} %copy-done.1, ...), custom_call_target="tpu_custom_call" | custom-call | flops 2415919104 | bytes 5242884 | tf_op jit(solution)/shard_map/pallas_call | solution.py:275
  91.1 3.6 %collective-permute-start.9 = (f32[2,256,256]{2,1,0:T(8,128)S(1)}, f32[2,256,256]{2,1,0:T(8,128)S(1)}, u32[]{:S(2)}, u32[]{:S(2)}) collective-permute-start(f32[2,256,256]{2,1,0:T(8,128)S(1)} %get-tuple-element.68), channel_id=1, source_target_pairs={{0,2},{1,3},{2,0},{3,1},{4,6},{5,7},{6,4},{7,5},{8,10},{9,11},{10,... | collective-permute-start | bytes 1572872 | tf_op jit(solution)/shard_map/ppermute | solution.py:295
  94.7 10.8 %collective-permute-done.8.pa_ref = f32[2,256,256]{2,1,0:T(8,128)S(1)} collective-permute-done((f32[2,256,256]{2,1,0:T(8,128)S(1)}, f32[2,256,256]{2,1,0:T(8,128)S(1)}, u32[]{:S(2)}, u32[]{:S(2)}) %collective-permute-start.8) | collective-permute-done | bytes 524320 | tf_op jit(solution)/shard_map/ppermute | solution.py:295
  106.8 9.0 %collective-permute-done.9.pb_ref = f32[2,256,256]{2,1,0:T(8,128)S(1)} collective-permute-done((f32[2,256,256]{2,1,0:T(8,128)S(1)}, f32[2,256,256]{2,1,0:T(8,128)S(1)}, u32[]{:S(2)}, u32[]{:S(2)}) %collective-permute-start.9) | collective-permute-done | bytes 524320 | tf_op jit(solution)/shard_map/ppermute | solution.py:295
  118.6 6.2 %collective-permute-start.12 = (f32[2,256,128]{2,1,0:T(8,128)S(1)}, f32[2,256,128]{2,1,0:T(8,128)S(1)}, u32[]{:S(2)}, u32[]{:S(2)}) collective-permute-start(f32[2,256,128]{2,1,0:T(8,128)S(1)} %get-tuple-element.69), channel_id=1, source_target_pairs={{2,4},{3,5},{4,2},{5,3},{6,8},{7,9},{8,6},{9,7},{10,12},{11,13},{1... | collective-permute-start | bytes 786440 | tf_op jit(solution)/shard_map/ppermute | solution.py:295
  124.9 6.8 %collective-permute-done.10.pr_ref = f32[2,256,128]{2,1,0:T(8,128)S(1)} collective-permute-done((f32[2,256,128]{2,1,0:T(8,128)S(1)}, f32[2,256,128]{2,1,0:T(8,128)S(1)}, u32[]{:S(2)}, u32[]{:S(2)}) %collective-permute-start.10) | collective-permute-done | bytes 262176 | tf_op jit(solution)/shard_map/ppermute | solution.py:295
  133.6 2.6 %shard_map.70 = (f32[2,256,256]{2,1,0:T(8,128)S(1)}, f32[2,256,256]{2,1,0:T(8,128)S(1)}, f32[2,256,256]{2,1,0:T(8,128)S(1)}, f32[2,256,640]{2,1,0:T(8,128)S(1)}) custom-call(s32[1]{0:T(128)} %bitcast.4.flag_ref, f32[2,256,256]{2,1,0:T(8,128)S(1)} %get-tuple-element.72.diag_ref, f32[2,256,256]{2,1,0:T(8,128)S(1)} %get-tuple-element.59.lower_ref, ...), custom_call_target="tpu_custom_call" | custom-call | flops 2295123200 | bytes 6291460 | tf_op jit(solution)/shard_map/pallas_call | solution.py:275
  136.2 4.3 %collective-permute-start.14 = (f32[2,256,640]{2,1,0:T(8,128)S(1)}, f32[2,256,640]{2,1,0:T(8,128)S(1)}, u32[]{:S(2)}, u32[]{:S(2)}) collective-permute-start(f32[2,256,640]{2,1,0:T(8,128)S(1)} %get-tuple-element.78), channel_id=1, source_target_pairs={{4,0},{5,1},{6,2},{7,3},{8,4},{9,5},{10,6},{11,7},{12,8},{13,9},{1... | collective-permute-start | bytes 3932168 | tf_op jit(solution)/shard_map/ppermute | solution.py:295
  141.9 24.8 %collective-permute-done.14.cr_ref = f32[2,256,640]{2,1,0:T(8,128)S(1)} collective-permute-done((f32[2,256,640]{2,1,0:T(8,128)S(1)}, f32[2,256,640]{2,1,0:T(8,128)S(1)}, u32[]{:S(2)}, u32[]{:S(2)}) %collective-permute-start.14) | collective-permute-done | bytes 1310752 | tf_op jit(solution)/shard_map/ppermute | solution.py:295
  167.9 3.1 %collective-permute-done.15.cl_ref = f32[2,256,640]{2,1,0:T(8,128)S(1)} collective-permute-done((f32[2,256,640]{2,1,0:T(8,128)S(1)}, f32[2,256,640]{2,1,0:T(8,128)S(1)}, u32[]{:S(2)}, u32[]{:S(2)}) %collective-permute-start.15) | collective-permute-done | bytes 1310752 | tf_op jit(solution)/shard_map/ppermute | solution.py:295
  170.9 2.9 %shard_map.72 = (f32[2,256,256]{2,1,0:T(8,128)S(1)}, f32[2,256,128]{2,1,0:T(8,128)S(1)}, f32[2,256,256]{2,1,0:T(8,128)S(1)}, f32[2,256,384]{2,1,0:T(8,128)S(1)}) custom-call(s32[1]{0:T(128)} %bitcast.5.flag_ref, f32[2,256,256]{2,1,0:T(8,128)S(1)} %get-tuple-element.79.diag_ref, f32[2,256,256]{2,1,0:T(8,128)S(1)} %get-tuple-element.80.lower_ref, ...), custom_call_target="tpu_custom_call" | custom-call | flops 2415919104 | bytes 5242884 | tf_op jit(solution)/shard_map/pallas_call | solution.py:275
  174.7 17.1 %collective-permute-done.16.coef_ref = f32[2,256,384]{2,1,0:T(8,128)S(1)} collective-permute-done((f32[2,256,384]{2,1,0:T(8,128)S(1)}, f32[2,256,384]{2,1,0:T(8,128)S(1)}, u32[]{:S(2)}, u32[]{:S(2)}) %collective-permute-start.16) | collective-permute-done | bytes 786464 | tf_op jit(solution)/shard_map/ppermute | solution.py:295
  191.7 2.7 %shard_map.73 = f32[2,256,128]{2,1,0:T(8,128)} custom-call(f32[2,256,256]{2,1,0:T(8,128)S(1)} %get-tuple-element.83.diag_ref, f32[2,256,128]{2,1,0:T(8,128)S(1)} %get-tuple-element.84.rhs_ref, f32[2,256,256]{2,1,0:T(8,128)S(1)} %get-tuple-element.85.w_ref, f32[2,256,384]{2,1,0:T(8,128)S(1)} %collective-permute-done.16.coef_ref), custom_call_target="tpu_custom_call" | custom-call | flops 1610612736 | bytes 2359296 | tf_op jit(solution)/shard_map/pallas_call | solution.py:275
  (47 shorter events, 24.2 us)
Async XLA Ops:
  2.3 8.7 %copy-start = (f32[2,256,256]{2,1,0:T(8,128)S(1)}, f32[2,256,256]{2,1,0:T(8,128)}, u32[]{:S(2)}) copy-start(f32[2,256,256]{2,1,0:T(8,128)} %upper_ref.1) | copy-start | bytes 1572868
  2.3 8.7 %copy-start.1 = (f32[2,256,256]{2,1,0:T(8,128)S(1)}, f32[2,256,256]{2,1,0:T(8,128)}, u32[]{:S(2)}) copy-start(f32[2,256,256]{2,1,0:T(8,128)} %lower_ref.1) | copy-start | bytes 1572868
  2.3 35.2 %all-to-all-start = ((f32[16,4,16,256]{3,2,1,0:T(8,128)}), f32[16,4,16,256]{3,2,1,0:T(8,128)S(1)}, u32[]{:S(2)}, u32[]{:S(2)}) async-start(f32[16,4,16,256]{3,2,1,0:T(8,128)} %copy_bitcast_fusion), calls=%async_computation | async-start | bytes 2097152 | tf_op jit(solution)/shard_map/all_to_all | solution.py:312
  11.9 27.1 %collective-permute-start.1 = (f32[2,256,256]{2,1,0:T(8,128)}, f32[2,256,256]{2,1,0:T(8,128)S(1)}, u32[]{:S(2)}, u32[]{:S(2)}) collective-permute-start(f32[2,256,256]{2,1,0:T(8,128)} %select_select_fusion), channel_id=1, source_target_pairs={{1,0},{2,1},{3,2},{4,3},{5,4},{6,5},{7,6},{8,7},{9,8},{10,9},{11,1... | collective-permute-start | bytes 1572872 | tf_op jit(solution)/shard_map/ppermute | solution.py:295
  17.1 21.9 %collective-permute-start = (f32[2,256,256]{2,1,0:T(8,128)}, f32[2,256,256]{2,1,0:T(8,128)}, u32[]{:S(2)}, u32[]{:S(2)}) collective-permute-start(f32[2,256,256]{2,1,0:T(8,128)} %select_select_fusion), channel_id=1, source_target_pairs={{0,1},{1,2},{2,3},{3,4},{4,5},{5,6},{6,7},{7,8},{8,9},{9,10},{10,1... | collective-permute-start | bytes 1572872 | tf_op jit(solution)/shard_map/ppermute | solution.py:295
  19.0 25.6 %copy-start.5 = (f32[2,1,256,128]{3,2,1,0:T(8,128)S(1)}, f32[2,1,256,128]{3,2,1,0:T(8,128)}, u32[]{:S(2)}) copy-start(f32[2,1,256,128]{3,2,1,0:T(8,128)} %param.11) | copy-start | bytes 786436
  19.0 44.6 %copy-start.2 = (f32[2,1,256,256]{3,2,1,0:T(8,128)S(1)}, f32[2,1,256,256]{3,2,1,0:T(8,128)}, u32[]{:S(2)}) copy-start(f32[2,1,256,256]{3,2,1,0:T(8,128)} %param.8) | copy-start | bytes 1572868
  39.0 24.6 %all-to-all-start.1 = ((f32[16,2,16,256]{3,2,1,0:T(8,128)}), f32[16,2,16,256]{3,2,1,0:T(8,128)S(1)}, u32[]{:S(2)}, u32[]{:S(2)}) async-start(f32[16,2,16,256]{3,2,1,0:T(8,128)} %convolve.1), calls=%async_computation.1 | async-start | bytes 1048576 | tf_op jit(solution)/shard_map/all_to_all | solution.py:318
  43.9 18.9 %collective-permute-start.2 = (f32[2,256,256]{2,1,0:T(8,128)}, f32[2,256,256]{2,1,0:T(8,128)S(1)}, u32[]{:S(2)}, u32[]{:S(2)}) collective-permute-start(f32[2,256,256]{2,1,0:T(8,128)} %collective-permute-done.hl_ref), channel_id=1, source_target_pairs={{0,16},{16,0},{32,48},{48,32},{64,80},{80,64},{96,112},{112,96},{1... | collective-permute-start | bytes 1572872 | tf_op jit(solution)/shard_map/ppermute | solution.py:320
  44.5 19.2 %collective-permute-start.3 = (f32[2,256,256]{2,1,0:T(8,128)S(1)}, f32[2,256,256]{2,1,0:T(8,128)S(1)}, u32[]{:S(2)}, u32[]{:S(2)}) collective-permute-start(f32[2,256,256]{2,1,0:T(8,128)S(1)} %collective-permute-done.1.hr_ref), channel_id=1, source_target_pairs={{0,16},{16,0},{32,48},{48,32},{64,80},{80,64},{96,112},{112,96},{1... | collective-permute-start | bytes 1572872 | tf_op jit(solution)/shard_map/ppermute | solution.py:321
  44.6 11.3 %collective-permute-start.5 = (f32[2,256,128]{2,1,0:T(8,128)S(1)}, f32[2,256,128]{2,1,0:T(8,128)S(1)}, u32[]{:S(2)}, u32[]{:S(2)}) collective-permute-start(f32[2,256,128]{2,1,0:T(8,128)S(1)} %bitcast.13), channel_id=1, source_target_pairs={{1,0},{2,1},{3,2},{4,3},{5,4},{6,5},{7,6},{8,7},{9,8},{10,9},{11,1... | collective-permute-start | bytes 786440 | tf_op jit(solution)/shard_map/ppermute | solution.py:295
  49.8 12.3 %collective-permute-start.4 = (f32[2,256,128]{2,1,0:T(8,128)S(1)}, f32[2,256,128]{2,1,0:T(8,128)S(1)}, u32[]{:S(2)}, u32[]{:S(2)}) collective-permute-start(f32[2,256,128]{2,1,0:T(8,128)S(1)} %bitcast.14), channel_id=1, source_target_pairs={{0,1},{1,2},{2,3},{3,4},{4,5},{5,6},{6,7},{7,8},{8,9},{9,10},{10,1... | collective-permute-start | bytes 786440 | tf_op jit(solution)/shard_map/ppermute | solution.py:295
  64.6 15.0 %collective-permute-start.6 = (f32[2,256,256]{2,1,0:T(8,128)S(1)}, f32[2,256,256]{2,1,0:T(8,128)S(1)}, u32[]{:S(2)}, u32[]{:S(2)}) collective-permute-start(f32[2,256,256]{2,1,0:T(8,128)S(1)} %get-tuple-element.54), channel_id=1, source_target_pairs={{1,0},{2,1},{3,2},{4,3},{5,4},{6,5},{7,6},{8,7},{9,8},{10,9},{11,1... | collective-permute-start | bytes 1572872 | tf_op jit(solution)/shard_map/ppermute | solution.py:295
  66.6 18.7 %collective-permute-start.7 = (f32[2,256,256]{2,1,0:T(8,128)S(1)}, f32[2,256,256]{2,1,0:T(8,128)S(1)}, u32[]{:S(2)}, u32[]{:S(2)}) collective-permute-start(f32[2,256,256]{2,1,0:T(8,128)S(1)} %get-tuple-element.54), channel_id=1, source_target_pairs={{0,1},{1,2},{2,3},{3,4},{4,5},{5,6},{6,7},{7,8},{8,9},{9,10},{10,1... | collective-permute-start | bytes 1572872 | tf_op jit(solution)/shard_map/ppermute | solution.py:295
  79.6 5.7 %copy-start.4 = (f32[2,256,256]{2,1,0:T(8,128)S(1)}, f32[2,256,256]{2,1,0:T(8,128)}, u32[]{:S(2)}) copy-start(f32[2,256,256]{2,1,0:T(8,128)} %copy-done.3) | copy-start | bytes 1572868
  89.1 16.4 %collective-permute-start.8 = (f32[2,256,256]{2,1,0:T(8,128)S(1)}, f32[2,256,256]{2,1,0:T(8,128)S(1)}, u32[]{:S(2)}, u32[]{:S(2)}) collective-permute-start(f32[2,256,256]{2,1,0:T(8,128)S(1)} %get-tuple-element.67), channel_id=1, source_target_pairs={{0,2},{1,3},{2,0},{3,1},{4,6},{5,7},{6,4},{7,5},{8,10},{9,11},{10,... | collective-permute-start | bytes 1572872 | tf_op jit(solution)/shard_map/ppermute | solution.py:295
  91.1 24.7 %collective-permute-start.9 = (f32[2,256,256]{2,1,0:T(8,128)S(1)}, f32[2,256,256]{2,1,0:T(8,128)S(1)}, u32[]{:S(2)}, u32[]{:S(2)}) collective-permute-start(f32[2,256,256]{2,1,0:T(8,128)S(1)} %get-tuple-element.68), channel_id=1, source_target_pairs={{0,2},{1,3},{2,0},{3,1},{4,6},{5,7},{6,4},{7,5},{8,10},{9,11},{10,... | collective-permute-start | bytes 1572872 | tf_op jit(solution)/shard_map/ppermute | solution.py:295
  105.5 27.3 %collective-permute-start.11 = (f32[2,256,256]{2,1,0:T(8,128)S(1)}, f32[2,256,256]{2,1,0:T(8,128)S(1)}, u32[]{:S(2)}, u32[]{:S(2)}) collective-permute-start(f32[2,256,256]{2,1,0:T(8,128)S(1)} %collective-permute-done.8.pa_ref), channel_id=1, source_target_pairs={{0,4},{1,5},{4,8},{5,9},{6,2},{7,3},{8,12},{9,13},{10,6},{11,7},{1... | collective-permute-start | bytes 1572872 | tf_op jit(solution)/shard_map/ppermute | solution.py:295
  115.8 17.8 %collective-permute-start.13 = (f32[2,256,256]{2,1,0:T(8,128)S(1)}, f32[2,256,256]{2,1,0:T(8,128)S(1)}, u32[]{:S(2)}, u32[]{:S(2)}) collective-permute-start(f32[2,256,256]{2,1,0:T(8,128)S(1)} %collective-permute-done.9.pb_ref), channel_id=1, source_target_pairs={{0,4},{1,5},{4,8},{5,9},{6,2},{7,3},{8,12},{9,13},{10,6},{11,7},{1... | collective-permute-start | bytes 1572872 | tf_op jit(solution)/shard_map/ppermute | solution.py:295
  117.1 14.6 %collective-permute-start.10 = (f32[2,256,128]{2,1,0:T(8,128)S(1)}, f32[2,256,128]{2,1,0:T(8,128)S(1)}, u32[]{:S(2)}, u32[]{:S(2)}) collective-permute-start(f32[2,256,128]{2,1,0:T(8,128)S(1)} %get-tuple-element.69), channel_id=1, source_target_pairs={{0,2},{1,3},{2,0},{3,1},{4,6},{5,7},{6,4},{7,5},{8,10},{9,11},{10,... | collective-permute-start | bytes 786440 | tf_op jit(solution)/shard_map/ppermute | solution.py:295
  118.6 14.2 %collective-permute-start.12 = (f32[2,256,128]{2,1,0:T(8,128)S(1)}, f32[2,256,128]{2,1,0:T(8,128)S(1)}, u32[]{:S(2)}, u32[]{:S(2)}) collective-permute-start(f32[2,256,128]{2,1,0:T(8,128)S(1)} %get-tuple-element.69), channel_id=1, source_target_pairs={{2,4},{3,5},{4,2},{5,3},{6,8},{7,9},{8,6},{9,7},{10,12},{11,13},{1... | collective-permute-start | bytes 786440 | tf_op jit(solution)/shard_map/ppermute | solution.py:295
  136.2 30.5 %collective-permute-start.14 = (f32[2,256,640]{2,1,0:T(8,128)S(1)}, f32[2,256,640]{2,1,0:T(8,128)S(1)}, u32[]{:S(2)}, u32[]{:S(2)}) collective-permute-start(f32[2,256,640]{2,1,0:T(8,128)S(1)} %get-tuple-element.78), channel_id=1, source_target_pairs={{4,0},{5,1},{6,2},{7,3},{8,4},{9,5},{10,6},{11,7},{12,8},{13,9},{1... | collective-permute-start | bytes 3932168 | tf_op jit(solution)/shard_map/ppermute | solution.py:295
  140.6 30.3 %collective-permute-start.15 = (f32[2,256,640]{2,1,0:T(8,128)S(1)}, f32[2,256,640]{2,1,0:T(8,128)S(1)}, u32[]{:S(2)}, u32[]{:S(2)}) collective-permute-start(f32[2,256,640]{2,1,0:T(8,128)S(1)} %get-tuple-element.78), channel_id=1, source_target_pairs={{0,4},{1,5},{2,6},{3,7},{4,8},{5,9},{6,10},{7,11},{8,12},{9,13},{1... | collective-permute-start | bytes 3932168 | tf_op jit(solution)/shard_map/ppermute | solution.py:295
  173.8 17.9 %collective-permute-start.16 = (f32[2,256,384]{2,1,0:T(8,128)S(1)}, f32[2,256,384]{2,1,0:T(8,128)S(1)}, u32[]{:S(2)}, u32[]{:S(2)}) collective-permute-start(f32[2,256,384]{2,1,0:T(8,128)S(1)} %get-tuple-element.86), channel_id=1, source_target_pairs={{0,8},{1,9},{2,10},{3,11},{4,12},{5,13},{6,14},{7,15},{8,0},{9,1},... | collective-permute-start | bytes 2359304 | tf_op jit(solution)/shard_map/ppermute | solution.py:295
  (5 other events, 10.0 us)

commit v3 on v2

--- a/solution.py
+++ b/solution.py
@@ -143,45 +143,46 @@
     save(inverse_ref, newton_inverse(diag))
 
 
-def level0_after_kernel(core_ref, diag_ref, upper_ref, xr_ref, hr_ref, or_ref, d_ref, tr_ref):
+def level0_after_kernel(
+    core_ref, diag_ref, upper_ref, xr_ref, hr_ref, or_ref, d_ref, u_ref, tr_ref
+):
     flag = core_ref[0] > 0
     after = multiply(left_side(load(upper_ref)), load(xr_ref))
     save(tr_ref, after)
-    z = multiply(left_side(after), choose(flag, load(hr_ref), load(or_ref)))
-    save(d_ref, minus(load(diag_ref), z))
+    left = left_side(after)
+    zh, zo = multiply(left, load(hr_ref)), multiply(left, load(or_ref))
+    save(d_ref, minus(load(diag_ref), choose(flag, zh, zo)))
+    save(u_ref, negative(choose(flag, zo, zh)))
 
 
 def level0_kernel(
-    core_ref, diag_ref, lower_ref, xl_ref, hl_ref, ol_ref,
-    d_ref, l_ref, alpha_ref, inverse_ref, tl_ref,
+    core_ref, diag_ref, lower_ref, upper_ref, xl_ref, hl_ref, ol_ref,
+    d_ref, beta_ref, inverse_ref, tl_ref,
 ):
     flag = core_ref[0] > 0
     before = multiply(left_side(load(lower_ref)), load(xl_ref))
     save(tl_ref, before)
-    left = left_side(before)
-    zh, zo = multiply(left, load(hl_ref)), multiply(left, load(ol_ref))
-    diag = minus(load(diag_ref), choose(flag, zo, zh))
-    new_lower = negative(choose(flag, zh, zo))
-    save(l_ref, new_lower)
+    z = multiply(left_side(before), choose(flag, load(ol_ref), load(hl_ref)))
+    diag = minus(load(diag_ref), z)
     save(d_ref, diag)
     inverse = newton_inverse(diag)
     save(inverse_ref, inverse)
-    save(alpha_ref, multiply(left_side(inverse), new_lower))
+    save(beta_ref, multiply(left_side(inverse), load(upper_ref)))
 
 
 def level0_rest_kernel(
-    core_ref, rhs_ref, inverse_ref, tl_ref, tr_ref, hr_ref, or_ref, rl_ref, rr_ref,
-    u_ref, r_ref, beta_ref, rho_ref,
+    core_ref, rhs_ref, inverse_ref, tl_ref, tr_ref, hl_ref, ol_ref, rl_ref, rr_ref,
+    l_ref, r_ref, alpha_ref, rho_ref,
 ):
     flag = core_ref[0] > 0
-    source = minus(load(rhs_ref), multiply(left_side(load(tl_ref)), load(rl_ref)))
-    after = left_side(load(tr_ref))
-    new_upper = negative(multiply(after, choose(flag, load(or_ref), load(hr_ref))))
-    source = minus(source, multiply(after, load(rr_ref)))
-    save(u_ref, new_upper)
+    before = left_side(load(tl_ref))
+    new_lower = negative(multiply(before, choose(flag, load(hl_ref), load(ol_ref))))
+    source = minus(load(rhs_ref), multiply(before, load(rl_ref)))
+    source = minus(source, multiply(left_side(load(tr_ref)), load(rr_ref)))
+    save(l_ref, new_lower)
     save(r_ref, source)
     left = left_side(load(inverse_ref))
-    save(beta_ref, multiply(left, new_upper))
+    save(alpha_ref, multiply(left, new_lower))
     save(rho_ref, multiply(left, source))
 
 
@@ -198,29 +199,29 @@
 
 
 def level1_middle_kernel(
-    flag_ref, diag_ref, lower_ref, upper_ref, rhs_ref, qa_ref, qr_ref, d_ref, q_ref, r_ref
+    flag_ref, diag_ref, lower_ref, upper_ref, rhs_ref, qb_ref, qr_ref, d_ref, q_ref, r_ref
 ):
     flag = flag_ref[0] > 0
+    left = left_side(choose(flag, load(lower_ref), load(upper_ref)))
+    zb = multiply(left, load(qb_ref))
+    diag = load(diag_ref)
+    save(d_ref, choose(flag, minus(diag, zb), diag))
+    save(q_ref, negative(zb))
+    save(r_ref, minus(load(rhs_ref), multiply(left, load(qr_ref))))
+
+
+def level1_kernel(
+    flag_ref, diag_ref, lower_ref, upper_ref, rhs_ref, p_ref, q_ref, qa_ref,
+    d_ref, l_ref, u_ref, coef_ref,
+):
+    flag = flag_ref[0] > 0
+    n = diag_ref.shape[1]
     left = left_side(choose(flag, load(lower_ref), load(upper_ref)))
     za = multiply(left, load(qa_ref))
     diag = load(diag_ref)
-    save(d_ref, choose(flag, diag, minus(diag, za)))
-    save(q_ref, negative(za))
-    save(r_ref, minus(load(rhs_ref), multiply(left, load(qr_ref))))
-
-
-def level1_kernel(
-    flag_ref, diag_ref, lower_ref, upper_ref, rhs_ref, p_ref, q_ref, qb_ref,
-    d_ref, l_ref, u_ref, coef_ref,
-):
-    flag = flag_ref[0] > 0
-    n = diag_ref.shape[1]
-    left = left_side(choose(flag, load(lower_ref), load(upper_ref)))
-    zb = multiply(left, load(qb_ref))
-    diag = load(diag_ref)
-    diag = choose(flag, minus(diag, zb), diag)
+    diag = choose(flag, diag, minus(diag, za))
     save(d_ref, diag)
-    new_p, new_q, source = load(p_ref), choose(flag, load(q_ref), negative(zb)), load(rhs_ref)
+    new_p, new_q, source = load(p_ref), choose(flag, negative(za), load(q_ref)), load(rhs_ref)
     new_upper, new_lower = choose(flag, new_p, new_q), choose(flag, new_q, new_p)
     save(l_ref, new_lower)
     save(u_ref, new_upper)
@@ -329,24 +330,24 @@
     diag, inverse = run(first_kernel, [square, square], [onsite, polar], 2)
     inverse_right = shift(inverse, -1)
     inverse_left = shift(inverse, 1)
-    diag, through_right = run(
+    diag, up, through_right = run(
         level0_after_kernel,
-        [square] * 2,
+        [square] * 3,
         [core_flag, diag, upper, inverse_right, half_right, other_right],
-        2,
-        1,
-    )
-    diag, low, alpha, inverse, through_left = run(
+        3,
+        1,
+    )
+    diag, beta, inverse, through_left = run(
         level0_kernel,
-        [square] * 5,
-        [core_flag, diag, lower, inverse_left, half_left, other_left],
-        6,
-        1,
-    )
-    up, source, beta, rho = run(
+        [square] * 4,
+        [core_flag, diag, lower, up, inverse_left, half_left, other_left],
+        5,
+        1,
+    )
+    low, source, alpha, rho = run(
         level0_rest_kernel,
         [square, tall, square, tall],
-        [core_flag, rhs, inverse, through_left, through_right, half_right, other_right, rhs_left, rhs_right],
+        [core_flag, rhs, inverse, through_left, through_right, half_left, other_left, rhs_left, rhs_right],
         3.5,
         1,
     )
@@ -369,14 +370,14 @@
     diag, mixed, source = run(
         level1_middle_kernel,
         [square, square, tall],
-        [right_first, diag, low, up, source, handed[0], handed[2]],
+        [right_first, diag, low, up, source, handed[1], handed[2]],
         1.7,
         1,
     )
     diag, low, up, coef = run(
         level1_kernel,
         [square, square, square, wide],
-        [right_first, diag, low, up, source, coupling, mixed, handed[1]],
+        [right_first, diag, low, up, source, coupling, mixed, handed[0]],
         5.7,
         1,
     )

time: 195 us -> 194 us (level)
  waiting for transfers between devices: 114 us -> 112 us
where the time goes in v3:
time: 194 us; the launch traced here: 193 us
  waiting for transfers between devices  112 us (58%)
  starting transfers between devices  54.8 us (28%)
  Pallas kernels  20 us (10%)
  other arithmetic  3.14 us (2%)
  local copies, waits for them, and re-layouts  2.24 us (1%)
    ppermute x15, waiting for transfers between devices, send(): return lax.ppermute(value, 'block', pairs)  94 us
    ppermute x15, starting transfers between devices, send(): return lax.ppermute(value, 'block', pairs)  40.6 us
    pallas_call x10, Pallas kernels, run(): pl.pallas_call(kernel, out_shape=outs, in_specs=specs, out_specs=[pl.Bloc...  18.5 us
    all_to_all x1, waiting for transfers between devices, program(): lax.all_to_all(pairs, 'energy', split_axis=0, concat_axis=0, tiled=True)  18.4 us
    all_to_all x1, starting transfers between devices, program(): lax.all_to_all(pairs, 'energy', split_axis=0, concat_axis=0, tiled=True)  8.7 us
    all_to_all x1, starting transfers between devices, program(): lax.all_to_all(polar, 'energy', split_axis=0, concat_axis=0, tiled=True)  4.93 us
  transfers between devices with their start and end apart: 19, of which 11 were waited for; matrix products, arithmetic and copies ran while one was open for 0% of the time, Pallas kernels for 4%

profile of v3, /device:TPU:6, one launch (start us, length us, event | category | flops | bytes accessed | tf_op | source)
XLA Modules:
  0.0 193.0 jit_solution(5147943830287568687)
XLA Ops:
  2.3 8.7 %all-to-all-start = ((f32[16,4,16,256]{3,2,1,0:T(8,128)}), f32[16,4,16,256]{3,2,1,0:T(8,128)S(1)}, u32[]{:S(2)}, u32[]{:S(2)}) async-start(f32[16,4,16,256]{3,2,1,0:T(8,128)} %copy_bitcast_fusion), calls=%async_computation | async-start | bytes 2097152 | tf_op jit(solution)/shard_map/all_to_all | solution.py:313
  11.9 5.2 %collective-permute-start.1 = (f32[2,256,256]{2,1,0:T(8,128)}, f32[2,256,256]{2,1,0:T(8,128)}, u32[]{:S(2)}, u32[]{:S(2)}) collective-permute-start(f32[2,256,256]{2,1,0:T(8,128)} %select_select_fusion), channel_id=1, source_target_pairs={{1,0},{2,1},{3,2},{4,3},{5,4},{6,5},{7,6},{8,7},{9,8},{10,9},{11,1... | collective-permute-start | bytes 1572872 | tf_op jit(solution)/shard_map/ppermute | solution.py:296
  19.0 18.4 %all-to-all-done.g_ref = f32[16,4,16,256]{3,2,1,0:T(8,128)S(1)} async-done(((f32[16,4,16,256]{3,2,1,0:T(8,128)}), f32[16,4,16,256]{3,2,1,0:T(8,128)S(1)}, u32[]{:S(2)}, u32[]{:S(2)}) %all-to-all-start) | async-done | bytes 1048608 | tf_op jit(solution)/shard_map/all_to_all | solution.py:313
  39.0 4.9 %all-to-all-start.1 = ((f32[16,2,16,256]{3,2,1,0:T(8,128)}), f32[16,2,16,256]{3,2,1,0:T(8,128)S(1)}, u32[]{:S(2)}, u32[]{:S(2)}) async-start(f32[16,2,16,256]{3,2,1,0:T(8,128)} %convolve.1), calls=%async_computation.1 | async-start | bytes 1048576 | tf_op jit(solution)/shard_map/all_to_all | solution.py:319
  44.6 5.2 %collective-permute-start.5 = (f32[2,256,128]{2,1,0:T(8,128)S(1)}, f32[2,256,128]{2,1,0:T(8,128)S(1)}, u32[]{:S(2)}, u32[]{:S(2)}) collective-permute-start(f32[2,256,128]{2,1,0:T(8,128)S(1)} %bitcast.13), channel_id=1, source_target_pairs={{1,0},{2,1},{3,2},{4,3},{5,4},{6,5},{7,6},{8,7},{9,8},{10,9},{11,1... | collective-permute-start | bytes 786440 | tf_op jit(solution)/shard_map/ppermute | solution.py:296
  51.7 4.2 %collective-permute-done.5.rr_ref = f32[2,256,128]{2,1,0:T(8,128)S(1)} collective-permute-done((f32[2,256,128]{2,1,0:T(8,128)S(1)}, f32[2,256,128]{2,1,0:T(8,128)S(1)}, u32[]{:S(2)}, u32[]{:S(2)}) %collective-permute-start.5) | collective-permute-done | bytes 262176 | tf_op jit(solution)/shard_map/ppermute | solution.py:296
  56.6 5.5 %collective-permute-done.4.rl_ref = f32[2,256,128]{2,1,0:T(8,128)S(1)} collective-permute-done((f32[2,256,128]{2,1,0:T(8,128)S(1)}, f32[2,256,128]{2,1,0:T(8,128)S(1)}, u32[]{:S(2)}, u32[]{:S(2)}) %collective-permute-start.4) | collective-permute-done | bytes 262176 | tf_op jit(solution)/shard_map/ppermute | solution.py:296
  66.6 3.9 %collective-permute-start.7 = (f32[2,256,256]{2,1,0:T(8,128)S(1)}, f32[2,256,256]{2,1,0:T(8,128)S(1)}, u32[]{:S(2)}, u32[]{:S(2)}) collective-permute-start(f32[2,256,256]{2,1,0:T(8,128)S(1)} %get-tuple-element.54), channel_id=1, source_target_pairs={{0,1},{1,2},{2,3},{3,4},{4,5},{5,6},{6,7},{7,8},{8,9},{9,10},{10,1... | collective-permute-start | bytes 1572872 | tf_op jit(solution)/shard_map/ppermute | solution.py:296
  70.5 9.1 %collective-permute-done.6.xr_ref = f32[2,256,256]{2,1,0:T(8,128)S(1)} collective-permute-done((f32[2,256,256]{2,1,0:T(8,128)S(1)}, f32[2,256,256]{2,1,0:T(8,128)S(1)}, u32[]{:S(2)}, u32[]{:S(2)}) %collective-permute-start.6) | collective-permute-done | bytes 524320 | tf_op jit(solution)/shard_map/ppermute | solution.py:296
  79.6 2.3 %shard_map.65 = (f32[2,256,256]{2,1,0:T(8,128)S(1)}, f32[2,256,256]{2,1,0:T(8,128)S(1)}, f32[2,256,256]{2,1,0:T(8,128)S(1)}) custom-call(s32[1]{0:T(128)} %bitcast.3.core_ref, f32[2,256,256]{2,1,0:T(8,128)S(1)} %get-tuple-element.53.diag_ref, f32[2,256,256]{2,1,0:T(8,128)S(1)} %copy-done, f32[2,256,256]{2,1,0:T(8,128)S(1)} %collective-permute-done.6.xr_ref, ...), custom_call_target="tpu_custom_call" | custom-call | flops 1207959552 | bytes 4194308 | tf_op jit(solution)/shard_map/pallas_call | solution.py:276
  82.0 3.3 %collective-permute-done.7.xl_ref = f32[2,256,256]{2,1,0:T(8,128)S(1)} collective-permute-done((f32[2,256,256]{2,1,0:T(8,128)S(1)}, f32[2,256,256]{2,1,0:T(8,128)S(1)}, u32[]{:S(2)}, u32[]{:S(2)}) %collective-permute-start.7) | collective-permute-done | bytes 524320 | tf_op jit(solution)/shard_map/ppermute | solution.py:296
  85.3 2.4 %shard_map.66 = (f32[2,256,256]{2,1,0:T(8,128)S(1)}, f32[2,256,256]{2,1,0:T(8,128)S(1)}, f32[2,256,256]{2,1,0:T(8,128)S(1)}, f32[2,256,256]{2,1,0:T(8,128)S(1)}) custom-call(s32[1]{0:T(128)} %bitcast.3.core_ref, f32[2,256,256]{2,1,0:T(8,128)S(1)} %get-tuple-element.56.diag_ref, f32[2,256,256]{2,1,0:T(8,128)S(1)} %copy-done.1, ...), custom_call_target="tpu_custom_call" | custom-call | flops 2013265920 | bytes 5242884 | tf_op jit(solution)/shard_map/pallas_call | solution.py:276
  89.4 3.6 %collective-permute-start.8 = (f32[2,256,256]{2,1,0:T(8,128)S(1)}, f32[2,256,256]{2,1,0:T(8,128)S(1)}, u32[]{:S(2)}, u32[]{:S(2)}) collective-permute-start(f32[2,256,256]{2,1,0:T(8,128)S(1)} %get-tuple-element.67), channel_id=1, source_target_pairs={{0,2},{1,3},{2,0},{3,1},{4,6},{5,7},{6,4},{7,5},{8,10},{9,11},{10,... | collective-permute-start | bytes 1572872 | tf_op jit(solution)/shard_map/ppermute | solution.py:296
  93.0 11.0 %collective-permute-done.9.pb_ref = f32[2,256,256]{2,1,0:T(8,128)S(1)} collective-permute-done((f32[2,256,256]{2,1,0:T(8,128)S(1)}, f32[2,256,256]{2,1,0:T(8,128)S(1)}, u32[]{:S(2)}, u32[]{:S(2)}) %collective-permute-start.9) | collective-permute-done | bytes 524320 | tf_op jit(solution)/shard_map/ppermute | solution.py:296
  105.3 9.0 %collective-permute-done.8.pa_ref = f32[2,256,256]{2,1,0:T(8,128)S(1)} collective-permute-done((f32[2,256,256]{2,1,0:T(8,128)S(1)}, f32[2,256,256]{2,1,0:T(8,128)S(1)}, u32[]{:S(2)}, u32[]{:S(2)}) %collective-permute-start.8) | collective-permute-done | bytes 524320 | tf_op jit(solution)/shard_map/ppermute | solution.py:296
  117.2 6.2 %collective-permute-start.12 = (f32[2,256,128]{2,1,0:T(8,128)S(1)}, f32[2,256,128]{2,1,0:T(8,128)S(1)}, u32[]{:S(2)}, u32[]{:S(2)}) collective-permute-start(f32[2,256,128]{2,1,0:T(8,128)S(1)} %get-tuple-element.69), channel_id=1, source_target_pairs={{2,4},{3,5},{4,2},{5,3},{6,8},{7,9},{8,6},{9,7},{10,12},{11,13},{1... | collective-permute-start | bytes 786440 | tf_op jit(solution)/shard_map/ppermute | solution.py:296
  123.4 6.8 %collective-permute-done.10.pr_ref = f32[2,256,128]{2,1,0:T(8,128)S(1)} collective-permute-done((f32[2,256,128]{2,1,0:T(8,128)S(1)}, f32[2,256,128]{2,1,0:T(8,128)S(1)}, u32[]{:S(2)}, u32[]{:S(2)}) %collective-permute-start.10) | collective-permute-done | bytes 262176 | tf_op jit(solution)/shard_map/ppermute | solution.py:296
  132.2 2.6 %shard_map.70 = (f32[2,256,256]{2,1,0:T(8,128)S(1)}, f32[2,256,256]{2,1,0:T(8,128)S(1)}, f32[2,256,256]{2,1,0:T(8,128)S(1)}, f32[2,256,640]{2,1,0:T(8,128)S(1)}) custom-call(s32[1]{0:T(128)} %bitcast.4.flag_ref, f32[2,256,256]{2,1,0:T(8,128)S(1)} %get-tuple-element.72.diag_ref, f32[2,256,256]{2,1,0:T(8,128)S(1)} %get-tuple-element.65.lower_ref, ...), custom_call_target="tpu_custom_call" | custom-call | flops 2295123200 | bytes 6291460 | tf_op jit(solution)/shard_map/pallas_call | solution.py:276
  134.8 4.3 %collective-permute-start.14 = (f32[2,256,640]{2,1,0:T(8,128)S(1)}, f32[2,256,640]{2,1,0:T(8,128)S(1)}, u32[]{:S(2)}, u32[]{:S(2)}) collective-permute-start(f32[2,256,640]{2,1,0:T(8,128)S(1)} %get-tuple-element.78), channel_id=1, source_target_pairs={{4,0},{5,1},{6,2},{7,3},{8,4},{9,5},{10,6},{11,7},{12,8},{13,9},{1... | collective-permute-start | bytes 3932168 | tf_op jit(solution)/shard_map/ppermute | solution.py:296
  140.4 24.8 %collective-permute-done.14.cr_ref = f32[2,256,640]{2,1,0:T(8,128)S(1)} collective-permute-done((f32[2,256,640]{2,1,0:T(8,128)S(1)}, f32[2,256,640]{2,1,0:T(8,128)S(1)}, u32[]{:S(2)}, u32[]{:S(2)}) %collective-permute-start.14) | collective-permute-done | bytes 1310752 | tf_op jit(solution)/shard_map/ppermute | solution.py:296
  166.4 3.1 %collective-permute-done.15.cl_ref = f32[2,256,640]{2,1,0:T(8,128)S(1)} collective-permute-done((f32[2,256,640]{2,1,0:T(8,128)S(1)}, f32[2,256,640]{2,1,0:T(8,128)S(1)}, u32[]{:S(2)}, u32[]{:S(2)}) %collective-permute-start.15) | collective-permute-done | bytes 1310752 | tf_op jit(solution)/shard_map/ppermute | solution.py:296
  169.5 2.9 %shard_map.72 = (f32[2,256,256]{2,1,0:T(8,128)S(1)}, f32[2,256,128]{2,1,0:T(8,128)S(1)}, f32[2,256,256]{2,1,0:T(8,128)S(1)}, f32[2,256,384]{2,1,0:T(8,128)S(1)}) custom-call(s32[1]{0:T(128)} %bitcast.5.flag_ref, f32[2,256,256]{2,1,0:T(8,128)S(1)} %get-tuple-element.79.diag_ref, f32[2,256,256]{2,1,0:T(8,128)S(1)} %get-tuple-element.80.lower_ref, ...), custom_call_target="tpu_custom_call" | custom-call | flops 2415919104 | bytes 5242884 | tf_op jit(solution)/shard_map/pallas_call | solution.py:276
  173.2 17.1 %collective-permute-done.16.coef_ref = f32[2,256,384]{2,1,0:T(8,128)S(1)} collective-permute-done((f32[2,256,384]{2,1,0:T(8,128)S(1)}, f32[2,256,384]{2,1,0:T(8,128)S(1)}, u32[]{:S(2)}, u32[]{:S(2)}) %collective-permute-start.16) | collective-permute-done | bytes 786464 | tf_op jit(solution)/shard_map/ppermute | solution.py:296
  190.3 2.7 %shard_map.73 = f32[2,256,128]{2,1,0:T(8,128)} custom-call(f32[2,256,256]{2,1,0:T(8,128)S(1)} %get-tuple-element.83.diag_ref, f32[2,256,128]{2,1,0:T(8,128)S(1)} %get-tuple-element.84.rhs_ref, f32[2,256,256]{2,1,0:T(8,128)S(1)} %get-tuple-element.85.w_ref, f32[2,256,384]{2,1,0:T(8,128)S(1)} %collective-permute-done.16.coef_ref), custom_call_target="tpu_custom_call" | custom-call | flops 1610612736 | bytes 2359296 | tf_op jit(solution)/shard_map/pallas_call | solution.py:276
  (47 shorter events, 25.3 us)
Async XLA Ops:
  2.3 8.7 %copy-start = (f32[2,256,256]{2,1,0:T(8,128)S(1)}, f32[2,256,256]{2,1,0:T(8,128)}, u32[]{:S(2)}) copy-start(f32[2,256,256]{2,1,0:T(8,128)} %upper_ref.1) | copy-start | bytes 1572868
  2.3 8.7 %copy-start.1 = (f32[2,256,256]{2,1,0:T(8,128)S(1)}, f32[2,256,256]{2,1,0:T(8,128)}, u32[]{:S(2)}) copy-start(f32[2,256,256]{2,1,0:T(8,128)} %lower_ref.1) | copy-start | bytes 1572868
  2.3 35.2 %all-to-all-start = ((f32[16,4,16,256]{3,2,1,0:T(8,128)}), f32[16,4,16,256]{3,2,1,0:T(8,128)S(1)}, u32[]{:S(2)}, u32[]{:S(2)}) async-start(f32[16,4,16,256]{3,2,1,0:T(8,128)} %copy_bitcast_fusion), calls=%async_computation | async-start | bytes 2097152 | tf_op jit(solution)/shard_map/all_to_all | solution.py:313
  11.9 27.1 %collective-permute-start.1 = (f32[2,256,256]{2,1,0:T(8,128)}, f32[2,256,256]{2,1,0:T(8,128)}, u32[]{:S(2)}, u32[]{:S(2)}) collective-permute-start(f32[2,256,256]{2,1,0:T(8,128)} %select_select_fusion), channel_id=1, source_target_pairs={{1,0},{2,1},{3,2},{4,3},{5,4},{6,5},{7,6},{8,7},{9,8},{10,9},{11,1... | collective-permute-start | bytes 1572872 | tf_op jit(solution)/shard_map/ppermute | solution.py:296
  17.1 21.9 %collective-permute-start = (f32[2,256,256]{2,1,0:T(8,128)}, f32[2,256,256]{2,1,0:T(8,128)S(1)}, u32[]{:S(2)}, u32[]{:S(2)}) collective-permute-start(f32[2,256,256]{2,1,0:T(8,128)} %select_select_fusion), channel_id=1, source_target_pairs={{0,1},{1,2},{2,3},{3,4},{4,5},{5,6},{6,7},{7,8},{8,9},{9,10},{10,1... | collective-permute-start | bytes 1572872 | tf_op jit(solution)/shard_map/ppermute | solution.py:296
  19.0 25.6 %copy-start.5 = (f32[2,1,256,128]{3,2,1,0:T(8,128)S(1)}, f32[2,1,256,128]{3,2,1,0:T(8,128)}, u32[]{:S(2)}) copy-start(f32[2,1,256,128]{3,2,1,0:T(8,128)} %param.11) | copy-start | bytes 786436
  19.0 44.6 %copy-start.2 = (f32[2,1,256,256]{3,2,1,0:T(8,128)S(1)}, f32[2,1,256,256]{3,2,1,0:T(8,128)}, u32[]{:S(2)}) copy-start(f32[2,1,256,256]{3,2,1,0:T(8,128)} %param.8) | copy-start | bytes 1572868
  39.0 24.6 %all-to-all-start.1 = ((f32[16,2,16,256]{3,2,1,0:T(8,128)}), f32[16,2,16,256]{3,2,1,0:T(8,128)S(1)}, u32[]{:S(2)}, u32[]{:S(2)}) async-start(f32[16,2,16,256]{3,2,1,0:T(8,128)} %convolve.1), calls=%async_computation.1 | async-start | bytes 1048576 | tf_op jit(solution)/shard_map/all_to_all | solution.py:319
  43.9 18.9 %collective-permute-start.3 = (f32[2,256,256]{2,1,0:T(8,128)}, f32[2,256,256]{2,1,0:T(8,128)S(1)}, u32[]{:S(2)}, u32[]{:S(2)}) collective-permute-start(f32[2,256,256]{2,1,0:T(8,128)} %collective-permute-done.1.hr_ref), channel_id=1, source_target_pairs={{0,16},{16,0},{32,48},{48,32},{64,80},{80,64},{96,112},{112,96},{1... | collective-permute-start | bytes 1572872 | tf_op jit(solution)/shard_map/ppermute | solution.py:322
  44.5 19.2 %collective-permute-start.2 = (f32[2,256,256]{2,1,0:T(8,128)S(1)}, f32[2,256,256]{2,1,0:T(8,128)S(1)}, u32[]{:S(2)}, u32[]{:S(2)}) collective-permute-start(f32[2,256,256]{2,1,0:T(8,128)S(1)} %collective-permute-done.hl_ref), channel_id=1, source_target_pairs={{0,16},{16,0},{32,48},{48,32},{64,80},{80,64},{96,112},{112,96},{1... | collective-permute-start | bytes 1572872 | tf_op jit(solution)/shard_map/ppermute | solution.py:321
  44.6 11.3 %collective-permute-start.5 = (f32[2,256,128]{2,1,0:T(8,128)S(1)}, f32[2,256,128]{2,1,0:T(8,128)S(1)}, u32[]{:S(2)}, u32[]{:S(2)}) collective-permute-start(f32[2,256,128]{2,1,0:T(8,128)S(1)} %bitcast.13), channel_id=1, source_target_pairs={{1,0},{2,1},{3,2},{4,3},{5,4},{6,5},{7,6},{8,7},{9,8},{10,9},{11,1... | collective-permute-start | bytes 786440 | tf_op jit(solution)/shard_map/ppermute | solution.py:296
  49.8 12.3 %collective-permute-start.4 = (f32[2,256,128]{2,1,0:T(8,128)S(1)}, f32[2,256,128]{2,1,0:T(8,128)S(1)}, u32[]{:S(2)}, u32[]{:S(2)}) collective-permute-start(f32[2,256,128]{2,1,0:T(8,128)S(1)} %bitcast.14), channel_id=1, source_target_pairs={{0,1},{1,2},{2,3},{3,4},{4,5},{5,6},{6,7},{7,8},{8,9},{9,10},{10,1... | collective-permute-start | bytes 786440 | tf_op jit(solution)/shard_map/ppermute | solution.py:296
  63.6 16.0 %copy-start.4 = (f32[2,256,256]{2,1,0:T(8,128)S(1)}, f32[2,256,256]{2,1,0:T(8,128)}, u32[]{:S(2)}) copy-start(f32[2,256,256]{2,1,0:T(8,128)} %copy-done.3) | copy-start | bytes 1572868
  64.6 15.0 %collective-permute-start.6 = (f32[2,256,256]{2,1,0:T(8,128)S(1)}, f32[2,256,256]{2,1,0:T(8,128)S(1)}, u32[]{:S(2)}, u32[]{:S(2)}) collective-permute-start(f32[2,256,256]{2,1,0:T(8,128)S(1)} %get-tuple-element.54), channel_id=1, source_target_pairs={{1,0},{2,1},{3,2},{4,3},{5,4},{6,5},{7,6},{8,7},{9,8},{10,9},{11,1... | collective-permute-start | bytes 1572872 | tf_op jit(solution)/shard_map/ppermute | solution.py:296
  66.6 18.7 %collective-permute-start.7 = (f32[2,256,256]{2,1,0:T(8,128)S(1)}, f32[2,256,256]{2,1,0:T(8,128)S(1)}, u32[]{:S(2)}, u32[]{:S(2)}) collective-permute-start(f32[2,256,256]{2,1,0:T(8,128)S(1)} %get-tuple-element.54), channel_id=1, source_target_pairs={{0,1},{1,2},{2,3},{3,4},{4,5},{5,6},{6,7},{7,8},{8,9},{9,10},{10,1... | collective-permute-start | bytes 1572872 | tf_op jit(solution)/shard_map/ppermute | solution.py:296
  87.7 16.4 %collective-permute-start.9 = (f32[2,256,256]{2,1,0:T(8,128)S(1)}, f32[2,256,256]{2,1,0:T(8,128)S(1)}, u32[]{:S(2)}, u32[]{:S(2)}) collective-permute-start(f32[2,256,256]{2,1,0:T(8,128)S(1)} %get-tuple-element.68), channel_id=1, source_target_pairs={{0,2},{1,3},{2,0},{3,1},{4,6},{5,7},{6,4},{7,5},{8,10},{9,11},{10,... | collective-permute-start | bytes 1572872 | tf_op jit(solution)/shard_map/ppermute | solution.py:296
  89.4 24.9 %collective-permute-start.8 = (f32[2,256,256]{2,1,0:T(8,128)S(1)}, f32[2,256,256]{2,1,0:T(8,128)S(1)}, u32[]{:S(2)}, u32[]{:S(2)}) collective-permute-start(f32[2,256,256]{2,1,0:T(8,128)S(1)} %get-tuple-element.67), channel_id=1, source_target_pairs={{0,2},{1,3},{2,0},{3,1},{4,6},{5,7},{6,4},{7,5},{8,10},{9,11},{10,... | collective-permute-start | bytes 1572872 | tf_op jit(solution)/shard_map/ppermute | solution.py:296
  104.1 27.3 %collective-permute-start.11 = (f32[2,256,256]{2,1,0:T(8,128)S(1)}, f32[2,256,256]{2,1,0:T(8,128)S(1)}, u32[]{:S(2)}, u32[]{:S(2)}) collective-permute-start(f32[2,256,256]{2,1,0:T(8,128)S(1)} %collective-permute-done.9.pb_ref), channel_id=1, source_target_pairs={{0,4},{1,5},{4,8},{5,9},{6,2},{7,3},{8,12},{9,13},{10,6},{11,7},{1... | collective-permute-start | bytes 1572872 | tf_op jit(solution)/shard_map/ppermute | solution.py:296
  114.4 17.8 %collective-permute-start.13 = (f32[2,256,256]{2,1,0:T(8,128)S(1)}, f32[2,256,256]{2,1,0:T(8,128)S(1)}, u32[]{:S(2)}, u32[]{:S(2)}) collective-permute-start(f32[2,256,256]{2,1,0:T(8,128)S(1)} %collective-permute-done.8.pa_ref), channel_id=1, source_target_pairs={{0,4},{1,5},{4,8},{5,9},{6,2},{7,3},{8,12},{9,13},{10,6},{11,7},{1... | collective-permute-start | bytes 1572872 | tf_op jit(solution)/shard_map/ppermute | solution.py:296
  115.7 14.6 %collective-permute-start.10 = (f32[2,256,128]{2,1,0:T(8,128)S(1)}, f32[2,256,128]{2,1,0:T(8,128)S(1)}, u32[]{:S(2)}, u32[]{:S(2)}) collective-permute-start(f32[2,256,128]{2,1,0:T(8,128)S(1)} %get-tuple-element.69), channel_id=1, source_target_pairs={{0,2},{1,3},{2,0},{3,1},{4,6},{5,7},{6,4},{7,5},{8,10},{9,11},{10,... | collective-permute-start | bytes 786440 | tf_op jit(solution)/shard_map/ppermute | solution.py:296
  117.2 14.2 %collective-permute-start.12 = (f32[2,256,128]{2,1,0:T(8,128)S(1)}, f32[2,256,128]{2,1,0:T(8,128)S(1)}, u32[]{:S(2)}, u32[]{:S(2)}) collective-permute-start(f32[2,256,128]{2,1,0:T(8,128)S(1)} %get-tuple-element.69), channel_id=1, source_target_pairs={{2,4},{3,5},{4,2},{5,3},{6,8},{7,9},{8,6},{9,7},{10,12},{11,13},{1... | collective-permute-start | bytes 786440 | tf_op jit(solution)/shard_map/ppermute | solution.py:296
  134.8 30.5 %collective-permute-start.14 = (f32[2,256,640]{2,1,0:T(8,128)S(1)}, f32[2,256,640]{2,1,0:T(8,128)S(1)}, u32[]{:S(2)}, u32[]{:S(2)}) collective-permute-start(f32[2,256,640]{2,1,0:T(8,128)S(1)} %get-tuple-element.78), channel_id=1, source_target_pairs={{4,0},{5,1},{6,2},{7,3},{8,4},{9,5},{10,6},{11,7},{12,8},{13,9},{1... | collective-permute-start | bytes 3932168 | tf_op jit(solution)/shard_map/ppermute | solution.py:296
  139.1 30.3 %collective-permute-start.15 = (f32[2,256,640]{2,1,0:T(8,128)S(1)}, f32[2,256,640]{2,1,0:T(8,128)S(1)}, u32[]{:S(2)}, u32[]{:S(2)}) collective-permute-start(f32[2,256,640]{2,1,0:T(8,128)S(1)} %get-tuple-element.78), channel_id=1, source_target_pairs={{0,4},{1,5},{2,6},{3,7},{4,8},{5,9},{6,10},{7,11},{8,12},{9,13},{1... | collective-permute-start | bytes 3932168 | tf_op jit(solution)/shard_map/ppermute | solution.py:296
  172.3 17.9 %collective-permute-start.16 = (f32[2,256,384]{2,1,0:T(8,128)S(1)}, f32[2,256,384]{2,1,0:T(8,128)S(1)}, u32[]{:S(2)}, u32[]{:S(2)}) collective-permute-start(f32[2,256,384]{2,1,0:T(8,128)S(1)} %get-tuple-element.86), channel_id=1, source_target_pairs={{0,8},{1,9},{2,10},{3,11},{4,12},{5,13},{6,14},{7,15},{8,0},{9,1},... | collective-permute-start | bytes 2359304 | tf_op jit(solution)/shard_map/ppermute | solution.py:296
  (5 other events, 7.2 us)
